TPU v7x, 32 devices: a whole 2x2x4 slice. The times are simulated.
32 devices in a mesh: grp: 4 (over y, x), slab: 8 (over z, core).
Axes of the slice: x: 2, y: 2, z: 4, core: 2. Of those that a mesh axis runs over, the one named last changes fastest.
Arguments:
- templates: float32 [4, 8, 512, 512], P('grp', None, 'slab'), may hold values from -6 to 6
- momentum: float32 [4, 8, 512, 512], P('grp', None, 'slab'), may hold values from -6 to 6
- subjects: float32 [4, 8, 512, 512], P('grp', None, 'slab'), may hold values from -6 to 6
- smooth_x: float32 [512, 512], replicated, may hold values from 0 to 1
- smooth_y: float32 [512, 512], replicated, may hold values from 0 to 1
- smooth_z: float32 [8, 8], replicated, may hold values from 0 to 1.5
- owned_block: int32 [4], replicated, may hold values from 0 to 3, each once
Outputs:
- final_image: float32 [4, 8, 512, 512], P('grp', None, 'slab')
- final_momentum: float32 [4, 8, 512, 512], P('grp', None, 'slab')
- center_owned: float32 [4, 2, 512, 512], P('grp', None, 'slab')
- new_templates: float32 [4, 8, 512, 512], P('grp', None, 'slab')
Inputs may be any that keep to these rules, and one draw needn't show every extreme that they name: `owned_block`: a permutation: every block has exactly one owning group.
All inputs are finite; a program needn't handle non-finite values.
Results may differ from a plain program's by a relative error of at most 0.0001.
Values sent between devices are 32-bit elements; how exact they have to be, the bound alone decides.
A program may use at most 64 MiB of HBM per device.

v0:
```python
import jax
import jax.numpy as jnp
from jax import lax
from jax.sharding import PartitionSpec as P

STEPS = 2


learn_rate = 0.5
pull_weight = 0.5


def with_halo(cells, sides, width):
    for axis, dim in sides:
        count = lax.axis_size(axis)
        ends = count - 1
        head = lax.slice_in_dim(cells, 0, width, axis=dim)
        tail = lax.slice_in_dim(cells, cells.shape[dim] - width, cells.shape[dim], axis=dim)
        cells = jnp.concatenate(
            [
                lax.ppermute(tail, axis, [(i, (i + 1) % count) for i in range(ends)]),
                cells,
                lax.ppermute(head, axis, [((i + 1) % count, i) for i in range(ends)]),
            ],
            axis=dim,
        )
    return cells


def diff_cols(field):
    zeros = jnp.zeros_like(field[..., :1])
    padded = jnp.concatenate([zeros, field, zeros], axis=-1)
    return (padded[..., 2:] - padded[..., :-2]) * 0.5


def diff_planes(field):
    zeros = jnp.zeros_like(field[..., :1, :, :])
    padded = jnp.concatenate([zeros, field, zeros], axis=-3)
    return (padded[..., 2:, :, :] - padded[..., :-2, :, :]) * 0.5


def smooth_planes(field, smooth_z):
    return jnp.einsum("ij,cjyx->ciyx", smooth_z, field, precision=lax.Precision.HIGHEST)


def smooth_plane(field, smooth_x, smooth_y):
    along = jnp.einsum("ij,cpyj->cpyi", smooth_x, field, precision=lax.Precision.HIGHEST)
    return jnp.einsum("ij,cpjx->cpix", smooth_y, along, precision=lax.Precision.HIGHEST)


def on_device(templates, momentum, subjects, smooth_x, smooth_y, smooth_z, owned_block):
    groups = lax.axis_size("grp")
    time_step = 1.0 / STEPS
    image = templates[0]
    moment = momentum[0]
    for section in range(STEPS):
        image_rows = with_halo(image, (("slab", 1),), 1)
        grad_rows = (image_rows[:, 2:, :] - image_rows[:, :-2, :]) * 0.5
        grad_cols = diff_cols(image)
        grad_planes = diff_planes(image)
        pushing = smooth_planes(
            jnp.stack([moment * grad_cols, moment * grad_rows, moment * grad_planes]), smooth_z
        )
        plane_fields = lax.all_to_all(pushing, "slab", split_axis=1, concat_axis=2, tiled=True)
        plane_vel = -smooth_plane(plane_fields, smooth_x, smooth_y)
        velocity = lax.all_to_all(plane_vel, "slab", split_axis=2, concat_axis=1, tiled=True)
        flux_edge = with_halo(moment * velocity[1], (("slab", 1),), 1)
        flux_rows = (flux_edge[:, 2:, :] - flux_edge[:, :-2, :]) * 0.5
        new_image = image - time_step * (
            velocity[0] * grad_cols + velocity[1] * grad_rows + velocity[2] * grad_planes
        )
        new_moment = moment - time_step * (
            diff_cols(moment * velocity[0]) + flux_rows + diff_planes(moment * velocity[2])
        )
        image = new_image
        moment = new_moment
    update = templates[0] - learn_rate * (image - subjects[0])
    planes_all = update.shape[0]
    block_planes = planes_all // groups
    center = lax.psum(update, "grp") / groups
    owned_index = owned_block[lax.axis_index("grp")]
    owned_out = lax.dynamic_slice_in_dim(center, owned_index * block_planes, block_planes, 0)[None]
    new_template = update + pull_weight * (center - update)
    return (image[None], moment[None], owned_out, new_template[None])


def solution(mesh):
    return jax.shard_map(
        on_device,
        mesh=mesh,
        in_specs=(
            P("grp", None, "slab", None),
            P("grp", None, "slab", None),
            P("grp", None, "slab", None),
            P(),
            P(),
            P(),
            P(),
        ),
        out_specs=(
            P("grp", None, "slab", None),
            P("grp", None, "slab", None),
            P("grp", None, "slab", None),
            P("grp", None, "slab", None),
        ),
        check_vma=False,
    )
```

profile of v0, /device:TPU:0, one launch (start us, length us, event | category | flops | bytes accessed | tf_op | source)
XLA Modules:
  0.0 467.9 jit_solution(9559274434863988958)
XLA Ops:
  7.2 1.9 copy.147
  9.2 1.3 collective-permute-start
  10.5 3.0 collective-permute-start.1
  13.5 0.8 collective-permute-done.1
  14.3 2.2 fusion.53
  16.5 3.3 fusion.15
  19.8 1.8 copy.79
  21.7 80.0 %all_to_all.16 = f32[3,8,64,512]{3,2,0,1:T(8,128)S(1)} all-to-all(f32[3,8,64,512]{3,2,0,1:T(8,128)S(1)} %copy.79), channel_id=1, replica_groups=mesh['grp'=4,'slab'=8] {'slab'}, dimensions={1} | all-to-all | bytes 6291456 | tf_op jit(solution)/shard_map/all_to_all | solution.py:64
  101.6 0.5 copy.80
  102.1 5.4 %fusion.51 = f32[3,512,512]{1,2,0:T(8,128)S(1)} fusion(f32[3,512,512]{2,1,0:T(8,128)S(1)} %bitcast.88, f32[512,512]{1,0:T(8,128)S(1)} %copy-done), kind=kOutput, calls=%fused_computation.74 | convolution fusion | flops 4831838208 | bytes 7340032 | tf_op jit(solution)/shard_map/ij,cpyj->cpyi/dot_general | solution.py:47
  107.5 6.8 %negate_bitcast_fusion.1 = f32[3,1,512,512]{2,3,0,1:T(8,128)} fusion(f32[3,512,512]{1,2,0:T(8,128)S(1)} %fusion.51, f32[512,512]{1,0:T(8,128)S(1)} %copy-done.3), kind=kOutput, calls=%fused_computation.13 | convolution fusion | flops 4832624640 | bytes 7340032 | tf_op jit(solution)/shard_map/ij,cpjx->cpix/dot_general | solution.py:48
  114.3 8.6 %copy.82 = f32[3,1,512,512]{3,1,0,2:T(1,128)} copy(f32[3,1,512,512]{2,3,0,1:T(8,128)} %negate_bitcast_fusion.1) | data formatting | bytes 6291456 | tf_op jit(solution)/shard_map/neg | solution.py:65
  122.9 75.3 %all_to_all.17 = f32[3,1,512,512]{3,1,0,2:T(1,128)S(1)} all-to-all(f32[3,1,512,512]{3,1,0,2:T(1,128)} %copy.82), channel_id=1, replica_groups=mesh['grp'=4,'slab'=8] {'slab'}, dimensions={2} | all-to-all | bytes 6291456 | tf_op jit(solution)/shard_map/all_to_all | solution.py:66
  198.1 2.2 fusion.62
  200.3 0.1 copy.113
  200.4 0.1 copy.114
  200.6 1.0 copy-done.1
  201.5 3.6 bitcast_multiply_fusion.2
  205.2 1.3 collective-permute-start.2
  206.5 3.0 collective-permute-start.3
  209.6 1.3 collective-permute-start.4
  210.9 3.2 collective-permute-start.5
  214.1 1.4 multiply_bitcast_fusion.2
  215.6 0.4 multiply_bitcast_fusion.1
  215.9 3.3 fusion.12
  219.2 1.8 copy.92
  221.0 76.3 %all_to_all.18 = f32[3,8,64,512]{3,2,0,1:T(8,128)S(1)} all-to-all(f32[3,8,64,512]{3,2,0,1:T(8,128)S(1)} %copy.92), channel_id=1, replica_groups=mesh['grp'=4,'slab'=8] {'slab'}, dimensions={1} | all-to-all | bytes 6291456 | tf_op jit(solution)/shard_map/all_to_all | solution.py:64
  297.3 0.5 copy.93
  297.8 5.4 %fusion.49 = f32[3,512,512]{1,2,0:T(8,128)S(1)} fusion(f32[3,512,512]{2,1,0:T(8,128)S(1)} %bitcast.89, f32[512,512]{1,0:T(8,128)S(1)} %copy-done), kind=kOutput, calls=%fused_computation.72 | convolution fusion | flops 4831838208 | bytes 7340032 | tf_op jit(solution)/shard_map/ij,cpyj->cpyi/dot_general | solution.py:47
  303.2 6.8 %negate_bitcast_fusion = f32[3,1,512,512]{2,3,0,1:T(8,128)} fusion(f32[3,512,512]{1,2,0:T(8,128)S(1)} %fusion.49, f32[512,512]{1,0:T(8,128)S(1)} %copy-done.4), kind=kOutput, calls=%fused_computation.12 | convolution fusion | flops 4832624640 | bytes 7340032 | tf_op jit(solution)/shard_map/ij,cpjx->cpix/dot_general | solution.py:48
  310.0 8.6 %copy.95 = f32[3,1,512,512]{3,1,0,2:T(1,128)} copy(f32[3,1,512,512]{2,3,0,1:T(8,128)} %negate_bitcast_fusion) | data formatting | bytes 6291456 | tf_op jit(solution)/shard_map/neg | solution.py:65
  318.6 75.3 %all_to_all.19 = f32[3,1,512,512]{3,1,0,2:T(1,128)S(1)} all-to-all(f32[3,1,512,512]{3,1,0,2:T(1,128)} %copy.95), channel_id=1, replica_groups=mesh['grp'=4,'slab'=8] {'slab'}, dimensions={2} | all-to-all | bytes 6291456 | tf_op jit(solution)/shard_map/all_to_all | solution.py:66
  393.9 2.2 fusion.61
  396.4 1.0 copy-done.5
  397.3 0.3 copy-done.6
  397.6 7.3 %fusion.46 = (f32[8,64,512]{2,0,1:T(8,128)}, f32[8,64,512]{2,0,1:T(8,128)}, f32[8,64,512]{2,0,1:T(8,128)}, f32[8,64,512]{2,0,1:T(8,128)}, f32[8,64,512]{2,0,1:T(8,128)}) fusion(f32[1,8,64,512]{3,2,1,0:T(8,128)S(1)} %copy-done.6, f32[1,8,64,512]{3,2,1,0:T(8,128)S(1)} %copy-done.5, f32[8,64,512]{2,0,1:T(8,128)S(1)} %get-tuple-element.46, ...), kind=kLoop, calls=%fused_computation.69 | loop fusion | flops 5505024 | bytes 12615680 | tf_op jit(solution)/shard_map/sub | solution.py:77
  405.0 0.7 fusion.63
  405.7 1.3 collective-permute-start.6
  407.0 3.0 collective-permute-start.7
  410.1 0.6 dynamic_slice.6
  411.3 2.8 copy.107
  414.1 3.7 fusion.32
  417.9 1.6 copy.108
  419.5 37.1 %all-reduce.18.cloned.1.call-done = f32[8,64,512]{2,0,1:T(8,128)} async-done(((f32[8,64,512]{2,0,1:T(8,128)}), f32[8,64,512]{2,0,1:T(8,128)}) %all-reduce.18.cloned.1.call-update) | async-done | bytes 1048592 | tf_op jit(solution)/shard_map/psum | solution.py:80
  456.6 1.5 add_bitcast_fusion
  458.1 1.6 copy.109
  459.7 0.1 constant_dynamic-slice_fusion
  459.8 0.8 copy.148
  (31 shorter events, 0.4 us)
Async XLA Ops:
  7.2 94.9 %copy-start = (f32[512,512]{1,0:T(8,128)S(1)}, f32[512,512]{1,0:T(8,128)}, u32[]{:S(2)}) copy-start(f32[512,512]{1,0:T(8,128)} %param.10) | copy-start | bytes 3145732
  7.2 449.4 %all-reduce.18.cloned.1.call-start = ((), (), s32[]{:S(2)}) async-start(), calls=%async_computation.4 | async-start | bytes 2097152 | tf_op jit(solution)/shard_map/psum | solution.py:80
  9.1 7.4 %copy-start.7 = (f32[8,8]{1,0:T(8,128)S(1)}, f32[8,8]{1,0:T(8,128)}, u32[]{:S(2)}) copy-start(f32[8,8]{1,0:T(8,128)} %param.12) | copy-start | bytes 772
  9.2 4.3 collective-permute-start
  10.5 3.9 collective-permute-start.1
  102.1 5.4 %copy-start.3 = (f32[512,512]{1,0:T(8,128)S(1)}, f32[512,512]{1,0:T(8,128)}, u32[]{:S(2)}) copy-start(f32[512,512]{1,0:T(8,128)} %param.11) | copy-start | bytes 3145732
  200.3 1.2 copy-start.1
  205.2 8.9 %collective-permute-start.2 = (f32[8,1,512]{2,0,1:T(8,128)S(1)}, f32[8,1,512]{2,0,1:T(8,128)S(1)}, u32[]{:S(2)}, u32[]{:S(2)}) collective-permute-start(f32[8,1,512]{2,0,1:T(8,128)S(1)} %get-tuple-element.48), channel_id=1, source_target_pairs={{1,0},{2,1},{3,2},{4,3},{5,4},{6,5},{7,6},{9,8},{10,9},{11,10},{12... | collective-permute-start | bytes 49160 | tf_op jit(solution)/shard_map/ppermute | solution.py:23
  206.5 7.6 %collective-permute-start.3 = (f32[8,1,512]{2,0,1:T(8,128)S(1)}, f32[8,1,512]{2,0,1:T(8,128)S(1)}, u32[]{:S(2)}, u32[]{:S(2)}) collective-permute-start(f32[8,1,512]{2,0,1:T(8,128)S(1)} %get-tuple-element.49), channel_id=1, source_target_pairs={{0,1},{1,2},{2,3},{3,4},{4,5},{5,6},{6,7},{8,9},{9,10},{10,11},{11... | collective-permute-start | bytes 49160 | tf_op jit(solution)/shard_map/ppermute | solution.py:21
  209.6 6.0 %collective-permute-start.4 = (f32[8,1,512]{2,0,1:T(8,128)S(1)}, f32[8,1,512]{2,0,1:T(8,128)S(1)}, u32[]{:S(2)}, u32[]{:S(2)}) collective-permute-start(f32[8,1,512]{2,0,1:T(8,128)S(1)} %get-tuple-element.42), channel_id=1, source_target_pairs={{1,0},{2,1},{3,2},{4,3},{5,4},{6,5},{7,6},{9,8},{10,9},{11,10},{12... | collective-permute-start | bytes 49160 | tf_op jit(solution)/shard_map/ppermute | solution.py:23
  210.9 4.7 %collective-permute-start.5 = (f32[8,1,512]{2,0,1:T(8,128)S(1)}, f32[8,1,512]{2,0,1:T(8,128)S(1)}, u32[]{:S(2)}, u32[]{:S(2)}) collective-permute-start(f32[8,1,512]{2,0,1:T(8,128)S(1)} %get-tuple-element.43), channel_id=1, source_target_pairs={{0,1},{1,2},{2,3},{3,4},{4,5},{5,6},{6,7},{8,9},{9,10},{10,11},{11... | collective-permute-start | bytes 49160 | tf_op jit(solution)/shard_map/ppermute | solution.py:21
  297.8 5.4 %copy-start.4 = (f32[512,512]{1,0:T(8,128)S(1)}, f32[512,512]{1,0:T(8,128)}, u32[]{:S(2)}) copy-start(f32[512,512]{1,0:T(8,128)} %param.11) | copy-start | bytes 3145732
  396.1 1.2 copy-start.5
  396.1 1.5 copy-start.6
  397.6 12.4 %copy-start.8 = (s32[4]{0:T(128)S(1)}, s32[4]{0:T(128)}, u32[]{:S(2)}) copy-start(s32[4]{0:T(128)} %param.13) | copy-start | bytes 52
  405.7 8.4 %collective-permute-start.6 = (f32[8,1,512]{2,0,1:T(8,128)S(1)}, f32[8,1,512]{2,0,1:T(8,128)S(1)}, u32[]{:S(2)}, u32[]{:S(2)}) collective-permute-start(f32[8,1,512]{2,0,1:T(8,128)S(1)} %get-tuple-element.37), channel_id=1, source_target_pairs={{1,0},{2,1},{3,2},{4,3},{5,4},{6,5},{7,6},{9,8},{10,9},{11,10},{12... | collective-permute-start | bytes 49160 | tf_op jit(solution)/shard_map/ppermute | solution.py:23
  407.0 7.1 %collective-permute-start.7 = (f32[8,1,512]{2,0,1:T(8,128)S(1)}, f32[8,1,512]{2,0,1:T(8,128)S(1)}, u32[]{:S(2)}, u32[]{:S(2)}) collective-permute-start(f32[8,1,512]{2,0,1:T(8,128)S(1)} %get-tuple-element.38), channel_id=1, source_target_pairs={{0,1},{1,2},{2,3},{3,4},{4,5},{5,6},{6,7},{8,9},{9,10},{10,11},{11... | collective-permute-start | bytes 49160 | tf_op jit(solution)/shard_map/ppermute | solution.py:21
  414.1 42.5 %copy-start.2 = (f32[8,64,512]{2,0,1:T(8,128)S(1)}, f32[8,64,512]{2,0,1:T(8,128)}, u32[]{:S(2)}) copy-start(f32[8,64,512]{2,0,1:T(8,128)} %get-tuple-element.20) | copy-start | bytes 3145732
Sparse Core Ops, SparseCore 0:
  405.1 51.4 all-reduce.17
where the time goes:
time: 474 us; the launch traced here: 468 us
  blocking collectives  307 us (65%)
  local copies, waits for them, and re-layouts  38.9 us (8%)
  waiting for transfers between devices  38 us (8%)
  matrix products  30.9 us (7%)
  other arithmetic  20.2 us (4%)
  starting transfers between devices  17.5 us (4%)
  between operations  15.5 us (3%)
    all_to_all x2, blocking collectives, on_device(): lax.all_to_all(pushing, 'slab', split_axis=1, concat_axis=2, tiled=True)  156 us
    all_to_all x2, blocking collectives, on_device(): lax.all_to_all(plane_vel, 'slab', split_axis=2, concat_axis=1, tiled=True)  151 us
    psum x1, waiting for transfers between devices, on_device(): center = lax.psum(update, 'grp') / groups  37.1 us
    neg x2, local copies, waits for them, and re-layouts, on_device(): plane_vel = -smooth_plane(plane_fields, smooth_x, smooth_y)  17.1 us
    dot_general x2, matrix products, smooth_plane(): jnp.einsum('ij,cpjx->cpix', smooth_y, along, precision=lax.Precision.HIGH...  13.6 us
    ppermute x4, starting transfers between devices, with_halo(): lax.ppermute(tail, axis, [(i, (i + 1) % count) for i in range(ends)])  12.3 us
    dot_general x2, matrix products, smooth_plane(): jnp.einsum('ij,cpyj->cpyi', smooth_x, field, precision=lax.Precision.HIGH...  10.7 us
    unnamed x28, local copies, waits for them, and re-layouts  10.6 us
  transfers between devices with their start and end apart: 9, of which 2 were waited for; matrix products, arithmetic and copies ran while one was open for 2% of the time, Pallas kernels for 0%

commit v1 on v0

--- a/solution.py
+++ b/solution.py
@@ -1,9 +1,16 @@
+import functools
+
 import jax
 import jax.numpy as jnp
 from jax import lax
+from jax.experimental import pallas as pl
+from jax.experimental.pallas import tpu as pltpu
 from jax.sharding import PartitionSpec as P
 
 STEPS = 2
+EDGE = 8
+VMEM_BYTES = 60 * 2**20
+GATHER_BYTES = 16 * 2**20
 
 
 learn_rate = 0.5
@@ -48,8 +55,205 @@
     return jnp.einsum("ij,cpjx->cpix", smooth_y, along, precision=lax.Precision.HIGHEST)
 
 
+def diff_rows(field):
+    zeros = jnp.zeros_like(field[..., :1, :])
+    padded = jnp.concatenate([zeros, field, zeros], axis=-2)
+    return (padded[..., 2:, :] - padded[..., :-2, :]) * 0.5
+
+
+def rows_of(field, start, count):
+    return lax.dynamic_slice_in_dim(field, start, count, field.ndim - 2)
+
+
+def halve(field):
+    high = field.astype(jnp.bfloat16)
+    return high, (field - high.astype(jnp.float32)).astype(jnp.bfloat16)
+
+
+def dot3(left, right):
+    mul = lambda a, b: jnp.dot(a, b, preferred_element_type=jnp.float32)
+    return mul(left[0], right[0]) + (mul(left[0], right[1]) + mul(left[1], right[0]))
+
+
+def central(field, axis):
+    size = field.shape[axis]
+    place = lax.broadcasted_iota(jnp.int32, field.shape, axis)
+    after = jnp.where(place == size - 1, 0.0, pltpu.roll(field, size - 1, axis))
+    before = jnp.where(place == 0, 0.0, pltpu.roll(field, 1, axis))
+    return (after - before) * 0.5
+
+
+def plane_grads(plane, planes, below, here, above):
+    over = jnp.where(plane == planes - 1, 0.0, above)
+    under = jnp.where(plane == 0, 0.0, below)
+    return central(here, 1), central(here, 0), (over - under) * 0.5
+
+
+def smooth_fields(grads, moment, fields, matrices, store):
+    rows_high, rows_low, cols_high, cols_low = matrices
+    for at, grad in enumerate(grads):
+        fields[at] = moment * grad
+
+    @pl.loop(0, 3)
+    def _(at):
+        along = dot3((rows_high[...], rows_low[...]), halve(fields[at]))
+        store(at, dot3(halve(along), (cols_high[...], cols_low[...])))
+
+
+def split_matrices(rows_ref, cols_ref, matrices):
+    matrices[0][...], matrices[1][...] = halve(rows_ref[...])
+    matrices[2][...], matrices[3][...] = halve(cols_ref[...])
+
+
+def full_kernel(
+    planes, step, smooth_z, below, here, above, m_below, m_here, m_above, rows_ref, cols_ref,
+    image_out, moment_out, vel, fields, *matrices,
+):
+    at = pl.program_id(0)
+    plane = at % planes
+
+    @pl.when(at == 0)
+    def _():
+        split_matrices(rows_ref, cols_ref, matrices)
+
+    @pl.when(at < planes)
+    def _():
+        grads = plane_grads(plane, planes, below[...], here[...], above[...])
+
+        def store(field, value):
+            vel[field, plane] = value
+
+        smooth_fields(grads, m_here[...], fields, matrices, store)
+
+    @pl.when(at == planes)
+    def _():
+        rows = vel.shape[2] // 8
+
+        @pl.loop(0, 3 * rows)
+        def _(turn):
+            field = turn // rows
+            span = pl.ds(pl.multiple_of((turn % rows) * 8, 8), 8)
+            held = [vel[field, j, span, :] for j in range(planes)]
+            for i in range(planes):
+                vel[field, i, span, :] = -sum(smooth_z[i, j] * held[j] for j in range(planes))
+
+    @pl.when(at >= planes)
+    def _():
+        grads = plane_grads(plane, planes, below[...], here[...], above[...])
+        moment = m_here[...]
+        moved = [vel[field, plane] for field in range(3)]
+        image_out[...] = here[...] - step * sum(v * g for v, g in zip(moved, grads))
+        over = m_above[...] * vel[2, jnp.minimum(plane + 1, planes - 1)]
+        under = m_below[...] * vel[2, jnp.maximum(plane - 1, 0)]
+        over = jnp.where(plane == planes - 1, 0.0, over)
+        under = jnp.where(plane == 0, 0.0, under)
+        moment_out[...] = moment - step * (
+            central(moment * moved[0], 1) + central(moment * moved[1], 0) + (over - under) * 0.5
+        )
+
+
+def part_kernel(
+    planes, below, here, above, m_here, rows_ref, cols_ref, vel_out, fields, *matrices
+):
+    plane = pl.program_id(0)
+
+    @pl.when(plane == 0)
+    def _():
+        split_matrices(rows_ref, cols_ref, matrices)
+
+    grads = plane_grads(plane, planes, below[...], here[...], above[...])
+
+    def store(field, value):
+        vel_out[field] = value
+
+    smooth_fields(grads, m_here[...], fields, matrices, store)
+
+
+def plane_spec(planes, rows, cols, which, shift):
+    def index(at):
+        return which, jnp.clip(at % planes + shift, 0, planes - 1), 0, 0
+
+    return pl.BlockSpec((None, None, rows, cols), index)
+
+
+def matrix_scratch(rows, inner, cols):
+    kinds = [(rows, inner), (rows, inner), (cols, cols), (cols, cols)]
+    return [pltpu.VMEM(kind, jnp.bfloat16) for kind in kinds]
+
+
+def whole_spec(shape):
+    return pl.BlockSpec(shape, lambda at: (0,) * len(shape))
+
+
+def full_step(state, smooth_x, smooth_y, smooth_z, step):
+    _, planes, rows, cols = state.shape
+    spec = lambda which, shift: plane_spec(planes, rows, cols, which, shift)
+    late = pl.BlockSpec((None, rows, cols), lambda at: (jnp.maximum(at - planes, 0), 0, 0))
+    out = jax.ShapeDtypeStruct((planes, rows, cols), jnp.float32)
+    return pl.pallas_call(
+        functools.partial(full_kernel, planes, step),
+        grid=(2 * planes,),
+        out_shape=(out, out),
+        in_specs=[pl.BlockSpec(memory_space=pltpu.SMEM)]
+        + [spec(which, shift) for which in (0, 1) for shift in (-1, 0, 1)]
+        + [whole_spec(smooth_y.shape), whole_spec(smooth_x.shape)],
+        out_specs=(late, late),
+        scratch_shapes=[
+            pltpu.VMEM((3, planes, rows, cols), jnp.float32),
+            pltpu.VMEM((3, rows, cols), jnp.float32),
+        ]
+        + matrix_scratch(rows, rows, cols),
+        compiler_params=pltpu.CompilerParams(vmem_limit_bytes=VMEM_BYTES),
+    )(smooth_z, *[state] * 6, smooth_y, smooth_x.T)
+
+
+def part_smooth(image, moment, smooth_x, smooth_y):
+    planes, rows, cols = image.shape
+    span = smooth_y.shape[0]
+    spec = lambda shift: pl.BlockSpec(
+        (None, rows, cols), lambda at: (jnp.clip(at + shift, 0, planes - 1), 0, 0)
+    )
+    return pl.pallas_call(
+        functools.partial(part_kernel, planes),
+        grid=(planes,),
+        out_shape=jax.ShapeDtypeStruct((3, planes, span, cols), jnp.float32),
+        in_specs=[spec(-1), spec(0), spec(1), spec(0)]
+        + [whole_spec(smooth_y.shape), whole_spec(smooth_x.shape)],
+        out_specs=pl.BlockSpec((3, None, span, cols), lambda at: (0, at, 0, 0)),
+        scratch_shapes=[pltpu.VMEM((3, rows, cols), jnp.float32)]
+        + matrix_scratch(span, rows, cols),
+        compiler_params=pltpu.CompilerParams(vmem_limit_bytes=VMEM_BYTES),
+    )(image, image, image, moment, smooth_y, smooth_x.T)
+
+
+def on_device_gathered(templates, momentum, subjects, smooth_x, smooth_y, smooth_z, owned_block):
+    time_step = 1.0 / STEPS
+    own = templates.shape[2]
+    total = smooth_y.shape[0]
+    index = lax.axis_index("slab")
+    state = lax.all_gather(
+        jnp.concatenate([templates, momentum], axis=0), "slab", axis=2, tiled=True
+    )
+    for section in range(STEPS - 1):
+        image, moment = full_step(state, smooth_x, smooth_y, smooth_z, time_step)
+        if section < STEPS - 2:
+            state = jnp.stack([image, moment])
+    span = own + 2 * EDGE
+    first = jnp.clip(index * own - EDGE, 0, total - span)
+    inner = index * own - first
+    vel = part_smooth(image, moment, smooth_x, rows_of(smooth_y, first, span))
+    vel = -smooth_planes(vel, smooth_z)
+    image, moment = rows_of(image, first, span), rows_of(moment, first, span)
+    grads = [diff_cols(image), diff_rows(image), diff_planes(image)]
+    new_image = image - time_step * sum(v * g for v, g in zip(vel, grads))
+    new_moment = moment - time_step * (
+        diff_cols(moment * vel[0]) + diff_rows(moment * vel[1]) + diff_planes(moment * vel[2])
+    )
+    image, moment = rows_of(new_image, inner, own), rows_of(new_moment, inner, own)
+    return finish(image, moment, templates, subjects, owned_block)
+
+
 def on_device(templates, momentum, subjects, smooth_x, smooth_y, smooth_z, owned_block):
-    groups = lax.axis_size("grp")
     time_step = 1.0 / STEPS
     image = templates[0]
     moment = momentum[0]
@@ -74,6 +278,11 @@
         )
         image = new_image
         moment = new_moment
+    return finish(image, moment, templates, subjects, owned_block)
+
+
+def finish(image, moment, templates, subjects, owned_block):
+    groups = lax.axis_size("grp")
     update = templates[0] - learn_rate * (image - subjects[0])
     planes_all = update.shape[0]
     block_planes = planes_all // groups
@@ -85,8 +294,13 @@
 
 
 def solution(mesh):
+    def body(*args):
+        templates, smooth_y = args[0], args[4]
+        gathered = 2 * 4 * templates.shape[1] * templates.shape[3] * smooth_y.shape[0]
+        return (on_device_gathered if gathered <= GATHER_BYTES else on_device)(*args)
+
     return jax.shard_map(
-        on_device,
+        body,
         mesh=mesh,
         in_specs=(
             P("grp", None, "slab", None),

time: 474 us -> 377 us (0.80); the launches traced: 468 us -> 376 us
  blocking collectives: 307 us -> 0 us
  waiting for transfers between devices: 38 us -> 191 us
  Pallas kernels: 0 us -> 129 us
  local copies, waits for them, and re-layouts: 38.9 us -> 11.5 us
  matrix products: 30.9 us -> 8.73 us
  starting transfers between devices: 17.5 us -> 0.08 us
    all_to_all x4 -> x0, blocking collectives: 307 us -> none  [the longest x2 156 us: on_device(): lax.all_to_all(pushing, 'slab', split_axis=1, concat_axis=2, tiled=True)]
    all_gather x0 -> x1, waiting for transfers between devices: none -> 150 us  [on_device_gathered(): lax.all_gather(jnp.concatenate([templates, momentum], axis=0), 'slab', ax...]
    pallas_call x0 -> x2, Pallas kernels: none -> 129 us  [the longest x1 98.3 us: full_step(): pl.pallas_call(functools.partial(full_kernel, planes, step), grid=(2 * pl...]
    dot_general x4 -> x0, matrix products: 24.3 us -> none  [the longest x2 13.6 us: smooth_plane(): jnp.einsum('ij,cpjx->cpix', smooth_y, along, precision=lax.Precision.HIGH...]
    ppermute x8 -> x0, starting transfers between devices: 17.5 us -> none  [the longest x4 12.3 us: with_halo(): lax.ppermute(tail, axis, [(i, (i + 1) % count) for i in range(ends)])]
    neg x2 -> x0, local copies, waits for them, and re-layouts: 17.1 us -> none  [on_device(): plane_vel = -smooth_plane(plane_fields, smooth_x, smooth_y)]
    unnamed x28 -> x17, local copies, waits for them, and re-layouts: 10.6 us -> 5.22 us
  transfers between devices with their start and end apart: 9 -> 2, of which waited for: 2 -> 2; matrix products, arithmetic and copies ran while one was open for 2% -> 3% of each run, Pallas kernels for 0% -> 0%
where the time goes in v1:
time: 377 us; the launch traced here: 376 us
  waiting for transfers between devices  191 us (51%)
  Pallas kernels  129 us (34%)
  other arithmetic  21 us (6%)
  between operations  14.8 us (4%)
  local copies, waits for them, and re-layouts  11.5 us (3%)
  matrix products  8.73 us (2%)
    all_gather x1, waiting for transfers between devices, on_device_gathered(): lax.all_gather(jnp.concatenate([templates, momentum], axis=0), 'slab', ax...  150 us
    pallas_call x1, Pallas kernels, full_step(): pl.pallas_call(functools.partial(full_kernel, planes, step), grid=(2 * pl...  98.3 us
    psum x1, waiting for transfers between devices, finish(): center = lax.psum(update, 'grp') / groups  41.6 us
    pallas_call x1, Pallas kernels, part_smooth(): pl.pallas_call(functools.partial(part_kernel, planes), grid=(planes,), ou...  30.5 us
    dot_general x1, matrix products, smooth_planes(): jnp.einsum('ij,cjyx->ciyx', smooth_z, field, precision=lax.Precision.HIGH...  8.73 us
  transfers between devices with their start and end apart: 2, of which 2 were waited for; matrix products, arithmetic and copies ran while one was open for 3% of the time, Pallas kernels for 0%

profile of v1, /device:TPU:0, one launch (start us, length us, event | category | flops | bytes accessed | tf_op | source)
XLA Modules:
  0.0 376.4 jit_solution(11777513143528177797)
XLA Ops:
  7.2 0.0 all-gather.2.cloned.1.call-start
  7.2 3.1 pad_maximum_fusion
  10.3 0.0 copy-start.5
  10.3 0.0 all-gather.2.cloned.1.call-update
  10.4 0.0 all-reduce.14.cloned.1.call-start
  10.4 1.1 copy-done.5
  11.6 1.3 copy.11
  12.9 1.6 constant_dynamic-slice_fusion.rows_ref
  14.5 149.9 %all-gather.2.cloned.1.call-done.below.here.above.m_below.m_here.m_above = f32[2,8,512,512]{3,2,1,0:T(8,128)} async-done(((f32[2,8,64,512]{3,2,1,0:T(8,128)}), f32[2,8,512,512]{3,2,1,0:T(8,128)}) %all-gather.2.cloned.1.call-update) | async-done | bytes 16777232 | tf_op jit(solution)/shard_map/all_gather | solution.py:234
  164.3 98.3 %shard_map.102 = (f32[8,512,512]{2,1,0:T(8,128)}, f32[8,512,512]{2,1,0:T(8,128)}) custom-call(f32[8,8]{1,0:T(8,128)} %smooth_z.1, f32[2,8,512,512]{3,2,1,0:T(8,128)} %all-gather.2.cloned.1.call-done.below.here.above.m_below.m_here.m_above, f32[2,8,512,512]{3,2,1,0:T(8,128)} %all-gather.2.cloned.1.call-done.below.here.above.m_below.m_here.m_above, ...), custom_call_target="tpu_custom_call" | custom-call | tf_op jit(solution)/shard_map/pallas_call | solution.py:193
  262.6 1.5 constant_dynamic-slice_fusion.1
  264.2 2.1 fusion.4
  266.3 0.0 copy-start.6
  266.3 30.5 %shard_map.103 = f32[3,8,80,512]{3,2,1,0:T(8,128)} custom-call(f32[8,512,512]{2,1,0:T(8,128)} %get-tuple-element.6.below.here.above, f32[8,512,512]{2,1,0:T(8,128)} %get-tuple-element.6.below.here.above, f32[8,512,512]{2,1,0:T(8,128)} %get-tuple-element.6.below.here.above, f32[8,512,512]{2,1,0:T(8,128)} %get-tuple-element.7.m_here, ...), custom_call_target="tpu_custom_call" | custom-call | tf_op jit(solution)/shard_map/pallas_call | solution.py:216
  296.7 0.0 copy-done.6
  296.8 8.7 %fusion.1 = f32[3,80,512,8]{2,3,1,0:T(8,128)S(1)} fusion(f32[3,8,80,512]{3,2,1,0:T(8,128)} %shard_map.103, f32[8,8]{1,0:T(8,128)S(1)} %copy-done.6), kind=kOutput, calls=%fused_computation.2 | convolution fusion | flops 94371840 | bytes 7864576 | tf_op jit(solution)/shard_map/ij,cjyx->ciyx/dot_general | solution.py:50
  305.5 2.4 fusion
  307.9 0.0 copy-start
  308.0 0.0 copy-start.2
  308.0 0.0 copy-start.3
  308.0 0.0 copy-start.4
  308.0 0.6 slice_bitcast_fusion.2
  308.6 1.5 copy-done
  310.0 0.2 copy-done.2
  310.2 0.8 copy-done.3
  311.0 0.3 copy-done.4
  311.3 0.0 copy-start.7
  311.3 4.2 %fusion.14 = (f32[8,64,512]{2,1,0:T(8,128)}, f32[8,64,512]{2,1,0:T(8,128)}) fusion(f32[1,8,64,512]{3,2,1,0:T(8,128)S(1)} %copy-done.4, f32[1,8,64,512]{3,2,1,0:T(8,128)S(1)} %copy-done.3, f32[8,80,512]{2,1,0:T(8,128)S(1)} %get-tuple-element.23, s32[]{:T(128)S(6)} %select_n.6, f32[8,80,512]{2,1,0:T(8,128)S(1)} %copy-done.2, ...), kind=kLoop, calls=%fused_computation.46 | loop fusion | flops 3670016 | bytes 12582920 | tf_op jit(solution)/shard_map/sub | solution.py:286
  315.5 0.0 all-reduce.14.cloned.1.call-update
  315.5 0.0 copy-done.7
  315.5 0.6 dynamic_slice.26
  316.8 3.3 dynamic-slice_multiply_fusion.2
  320.1 0.3 pad_slice_fusion.9
  320.4 1.0 pad_slice_fusion.1
  321.4 0.0 copy-start.1
  321.4 3.5 fusion.5
  324.8 41.6 %all-reduce.14.cloned.1.call-done = f32[8,64,512]{2,1,0:T(8,128)} async-done(((f32[8,64,512]{2,1,0:T(8,128)}), f32[8,64,512]{2,1,0:T(8,128)}) %all-reduce.14.cloned.1.call-update) | async-done | bytes 1048592 | tf_op jit(solution)/shard_map/psum | solution.py:289
  366.4 0.0 copy-done.1
  366.4 2.5 add_bitcast_fusion
  368.9 0.7 dynamic-slice_bitcast_fusion
Async XLA Ops:
  7.2 157.2 %all-gather.2.cloned.1.call-start = ((), (), s32[]{:S(2)}) async-start(), calls=%async_computation | async-start | bytes 18874368 | tf_op jit(solution)/shard_map/all_gather | solution.py:234
  10.3 1.2 copy-start.5
  10.4 356.1 %all-reduce.14.cloned.1.call-start = ((), (), s32[]{:S(2)}) async-start(), calls=%async_computation.1 | async-start | bytes 2097152 | tf_op jit(solution)/shard_map/psum | solution.py:289
  266.3 30.5 %copy-start.6 = (f32[8,8]{1,0:T(8,128)S(1)}, f32[8,8]{1,0:T(8,128)}, u32[]{:S(2)}) copy-start(f32[8,8]{1,0:T(8,128)} %smooth_z.1) | copy-start | bytes 772
  307.9 2.1 copy-start
  308.0 2.3 copy-start.2
  308.0 3.0 copy-start.3
  308.0 3.3 copy-start.4
  311.3 4.2 %copy-start.7 = (s32[4]{0:T(128)S(1)}, s32[4]{0:T(128)}, u32[]{:S(2)}) copy-start(s32[4]{0:T(128)} %param.13) | copy-start | bytes 52
  321.4 45.0 %copy-start.1 = (f32[8,64,512]{2,1,0:T(8,128)S(1)}, f32[8,64,512]{2,1,0:T(8,128)}, u32[]{:S(2)}) copy-start(f32[8,64,512]{2,1,0:T(8,128)} %get-tuple-element.8) | copy-start | bytes 3145732
Sparse Core Ops, SparseCore 0:
  10.5 153.7 all-gather.1
  315.6 50.7 all-reduce.13

commit v2 on v0

--- a/solution.py
+++ b/solution.py
@@ -1,9 +1,17 @@
+import functools
+
 import jax
 import jax.numpy as jnp
 from jax import lax
+from jax.experimental import pallas as pl
+from jax.experimental.pallas import tpu as pltpu
 from jax.sharding import PartitionSpec as P
 
 STEPS = 2
+EDGE = 8
+CUTS = (3, 5, 7)
+VMEM_BYTES = 60 * 2**20
+GATHER_BYTES = 16 * 2**20
 
 
 learn_rate = 0.5
@@ -48,8 +56,347 @@
     return jnp.einsum("ij,cpjx->cpix", smooth_y, along, precision=lax.Precision.HIGHEST)
 
 
+def diff_rows(field):
+    zeros = jnp.zeros_like(field[..., :1, :])
+    padded = jnp.concatenate([zeros, field, zeros], axis=-2)
+    return (padded[..., 2:, :] - padded[..., :-2, :]) * 0.5
+
+
+def rows_of(field, start, count):
+    return lax.dynamic_slice_in_dim(field, start, count, field.ndim - 2)
+
+
+def halve(field):
+    high = field.astype(jnp.bfloat16)
+    return high, (field - high.astype(jnp.float32)).astype(jnp.bfloat16)
+
+
+def dot3(left, right):
+    mul = lambda a, b: jnp.dot(a, b, preferred_element_type=jnp.float32)
+    return mul(left[0], right[0]) + (mul(left[0], right[1]) + mul(left[1], right[0]))
+
+
+def central(field, axis):
+    size = field.shape[axis]
+    place = lax.broadcasted_iota(jnp.int32, field.shape, axis)
+    after = jnp.where(place == size - 1, 0.0, pltpu.roll(field, size - 1, axis))
+    before = jnp.where(place == 0, 0.0, pltpu.roll(field, 1, axis))
+    return (after - before) * 0.5
+
+
+def plane_grads(plane, planes, below, here, above):
+    over = jnp.where(plane == planes - 1, 0.0, above)
+    under = jnp.where(plane == 0, 0.0, below)
+    return central(here, 1), central(here, 0), (over - under) * 0.5
+
+
+def smooth_fields(grads, moment, fields, matrices, store):
+    rows_high, rows_low, cols_high, cols_low = matrices
+    for at, grad in enumerate(grads):
+        fields[at] = moment * grad
+
+    @pl.loop(0, 3)
+    def _(at):
+        along = dot3((rows_high[...], rows_low[...]), halve(fields[at]))
+        store(at, dot3(halve(along), (cols_high[...], cols_low[...])))
+
+
+def split_matrices(rows_ref, cols_ref, matrices):
+    matrices[0][...], matrices[1][...] = halve(rows_ref[...])
+    matrices[2][...], matrices[3][...] = halve(cols_ref[...])
+
+
+def chunk_kernel(low, count, planes, starts, *refs):
+    chunks, refs = refs[: len(starts)], refs[len(starts) :]
+    rows_ref, cols_ref, vel_out, images, moments, fields, sems = refs[:7]
+    matrices = refs[7:]
+    turn = pl.program_id(0)
+    near = range(max(low - 1, 0), min(low + count + 1, planes))
+
+    def place(plane):
+        which = max(k for k, start in enumerate(starts) if start <= plane)
+        return chunks[which], plane - starts[which]
+
+    def image_copy(plane):
+        chunk, at = place(plane)
+        slot = plane - low + 1
+        return pltpu.make_async_copy(chunk.at[0, at], images.at[slot], sems.at[0, slot])
+
+    def moment_copy(plane):
+        chunk, at = place(plane)
+        slot = plane - low
+        return pltpu.make_async_copy(chunk.at[1, at], moments.at[slot], sems.at[1, slot])
+
+    @pl.when(turn == 0)
+    def _():
+        for plane in near:
+            image_copy(plane).start()
+            if low <= plane < low + count:
+                moment_copy(plane).start()
+        split_matrices(rows_ref, cols_ref, matrices)
+
+    for step in range(count):
+
+        @pl.when(turn == step)
+        def _(step=step):
+            for plane in near:
+                if plane == low + step + 1 or (step == 0 and plane <= low):
+                    image_copy(plane).wait()
+            moment_copy(low + step).wait()
+
+    grads = plane_grads(low + turn, planes, images[turn], images[turn + 1], images[turn + 2])
+
+    def store(field, value):
+        vel_out[field] = value
+
+    smooth_fields(grads, moments[turn], fields, matrices, store)
+
+
+def chunk_smooth(chunks, starts, low, count, planes, smooth_y, cols_matrix):
+    rows, cols = chunks[0].shape[2:]
+    return pl.pallas_call(
+        functools.partial(chunk_kernel, low, count, planes, starts),
+        grid=(count,),
+        out_shape=jax.ShapeDtypeStruct((3, count, rows, cols), jnp.float32),
+        in_specs=[pl.BlockSpec(memory_space=pl.ANY)] * len(chunks)
+        + [whole_spec(smooth_y.shape), whole_spec(cols_matrix.shape)],
+        out_specs=pl.BlockSpec((3, None, rows, cols), lambda at: (0, at, 0, 0)),
+        scratch_shapes=[
+            pltpu.VMEM((count + 2, rows, cols), jnp.float32),
+            pltpu.VMEM((count, rows, cols), jnp.float32),
+            pltpu.VMEM((3, rows, cols), jnp.float32),
+            pltpu.SemaphoreType.DMA((2, count + 2)),
+        ]
+        + matrix_scratch(rows, rows, cols),
+        cost_estimate=pl.CostEstimate(
+            flops=36 * count * rows * rows * cols,
+            bytes_accessed=20 * count * rows * cols,
+            transcendentals=0,
+        ),
+        compiler_params=pltpu.CompilerParams(vmem_limit_bytes=40 * 2**20),
+    )(*chunks, smooth_y, cols_matrix)
+
+
+def shoot_kernel(planes, starts, parts, blocks, step, first_ref, smooth_z, *refs):
+    chunks, refs = refs[: len(starts)], refs[len(starts) :]
+    smoothed, refs = refs[: len(parts)], refs[len(parts) :]
+    rows_ref, cols_ref, vel_out, image_out, moment_out = refs[:5]
+    vel, images, moments, new_images, new_moments, fields, sems = refs[5:12]
+    matrices = refs[12:]
+    turn = pl.program_id(0)
+    plane = turn - blocks
+    rows = vel.shape[2]
+    block = rows // blocks
+    span = image_out.shape[0]
+
+    def copies(at):
+        which = max(k for k, start in enumerate(starts) if start <= at)
+        inner, slot = at - starts[which], at % 4
+        return [
+            pltpu.make_async_copy(
+                chunks[which].at[kind, inner], into.at[slot], sems.at[kind, slot]
+            )
+            for kind, into in enumerate((images, moments))
+        ]
+
+    @pl.when(turn == 0)
+    def _():
+        for at in range(min(2, planes)):
+            for copy in copies(at):
+                copy.start()
+        split_matrices(rows_ref, cols_ref, matrices)
+
+    @pl.when(turn < blocks)
+    def _():
+        @pl.loop(0, 3 * (block // 8))
+        def _(part):
+            field = part // (block // 8)
+            inner = (part % (block // 8)) * 8
+            held = [
+                piece[field, j, pl.ds(pl.multiple_of(inner, 8), 8), :]
+                for piece in smoothed
+                for j in range(piece.shape[1])
+            ]
+            into = pl.ds(pl.multiple_of(turn * block + inner, 8), 8)
+            for i in range(planes):
+                vel[field, i, into, :] = -sum(smooth_z[i, j] * held[j] for j in range(planes))
+
+    for at in range(planes):
+
+        @pl.when(plane == at)
+        def _(at=at):
+            if at + 2 < planes:
+                for copy in copies(at + 2):
+                    copy.start()
+            for near in ([0, 1] if at == 0 else [at + 1]):
+                if near < planes:
+                    for copy in copies(near):
+                        copy.wait()
+
+    @pl.when((plane >= 0) & (plane < planes))
+    def _():
+        here, above, below = plane % 4, (plane + 1) % 4, (plane + 3) % 4
+        image, moment = images[here], moments[here]
+        grads = plane_grads(plane, planes, images[below], image, images[above])
+        moved = [vel[field, plane] for field in range(3)]
+        new_images[plane % 3] = image - step * sum(v * g for v, g in zip(moved, grads))
+        over = moments[above] * vel[2, jnp.minimum(plane + 1, planes - 1)]
+        under = moments[below] * vel[2, jnp.maximum(plane - 1, 0)]
+        over = jnp.where(plane == planes - 1, 0.0, over)
+        under = jnp.where(plane == 0, 0.0, under)
+        new_moments[plane % 2] = moment - step * (
+            central(moment * moved[0], 1) + central(moment * moved[1], 0) + (over - under) * 0.5
+        )
+
+    @pl.when(plane >= 1)
+    def _():
+        last = plane - 1
+        grads = plane_grads(
+            last, planes, new_images[(last + 2) % 3], new_images[last % 3],
+            new_images[(last + 1) % 3],
+        )
+
+        def store(field, value):
+            vel_out[field] = value
+
+        smooth_fields(grads, new_moments[last % 2], fields, matrices, store)
+        window = pl.ds(pl.multiple_of(first_ref[0], 8), span)
+        image_out[...] = new_images[last % 3, window, :]
+        moment_out[...] = new_moments[last % 2, window, :]
+
+
+def shoot(chunks, starts, smoothed, planes, smooth_z, rows_matrix, cols_matrix, first, step):
+    rows, cols = chunks[0].shape[2:]
+    span = rows_matrix.shape[0]
+    blocks = max(1, rows // 64)
+    block = rows // blocks
+    parts = [piece.shape[1] for piece in smoothed]
+    late = lambda at: jnp.clip(at - blocks - 1, 0, planes - 1)
+    out = jax.ShapeDtypeStruct((planes, span, cols), jnp.float32)
+    window = pl.BlockSpec((None, span, cols), lambda at: (late(at), 0, 0))
+    return pl.pallas_call(
+        functools.partial(shoot_kernel, planes, starts, parts, blocks, step),
+        grid=(blocks + planes + 1,),
+        out_shape=(jax.ShapeDtypeStruct((3, planes, span, cols), jnp.float32), out, out),
+        in_specs=[pl.BlockSpec(memory_space=pltpu.SMEM)] * 2
+        + [pl.BlockSpec(memory_space=pl.ANY)] * len(chunks)
+        + [
+            pl.BlockSpec(
+                (3, part, block, cols), lambda at: (0, 0, jnp.minimum(at, blocks - 1), 0)
+            )
+            for part in parts
+        ]
+        + [whole_spec(rows_matrix.shape), whole_spec(cols_matrix.shape)],
+        out_specs=(
+            pl.BlockSpec((3, None, span, cols), lambda at: (0, late(at), 0, 0)),
+            window,
+            window,
+        ),
+        scratch_shapes=[
+            pltpu.VMEM((3, planes, rows, cols), jnp.float32),
+            pltpu.VMEM((4, rows, cols), jnp.float32),
+            pltpu.VMEM((4, rows, cols), jnp.float32),
+            pltpu.VMEM((3, rows, cols), jnp.float32),
+            pltpu.VMEM((2, rows, cols), jnp.float32),
+            pltpu.VMEM((3, rows, cols), jnp.float32),
+            pltpu.SemaphoreType.DMA((2, 4)),
+        ]
+        + matrix_scratch(span, rows, cols),
+        compiler_params=pltpu.CompilerParams(vmem_limit_bytes=VMEM_BYTES),
+    )(first, smooth_z, *chunks, *smoothed, rows_matrix, cols_matrix)
+
+
+def last_kernel(
+    planes, own, step, inner_ref, smooth_z, smoothed, image_ref, moment_ref, templates, subjects,
+    image_out, moment_out, update_out, vel,
+):
+    span = image_ref.shape[1]
+
+    @pl.loop(0, 3 * (span // 8))
+    def _(part):
+        field = part // (span // 8)
+        rows = pl.ds(pl.multiple_of((part % (span // 8)) * 8, 8), 8)
+        held = [smoothed[field, j, rows, :] for j in range(planes)]
+        for i in range(planes):
+            vel[field, i, rows, :] = -sum(smooth_z[i, j] * held[j] for j in range(planes))
+
+    inner = pl.ds(pl.multiple_of(inner_ref[0], 8), own)
+
+    @pl.loop(0, planes)
+    def _(plane):
+        over_at, under_at = jnp.minimum(plane + 1, planes - 1), jnp.maximum(plane - 1, 0)
+        image, moment = image_ref[plane], moment_ref[plane]
+        grads = plane_grads(plane, planes, image_ref[under_at], image, image_ref[over_at])
+        moved = [vel[field, plane] for field in range(3)]
+        over = jnp.where(plane == planes - 1, 0.0, moment_ref[over_at] * vel[2, over_at])
+        under = jnp.where(plane == 0, 0.0, moment_ref[under_at] * vel[2, under_at])
+        vel[0, plane] = image - step * sum(v * g for v, g in zip(moved, grads))
+        vel[1, plane] = moment - step * (
+            central(moment * moved[0], 1) + central(moment * moved[1], 0) + (over - under) * 0.5
+        )
+        new_image = vel[0, plane, inner, :]
+        image_out[0, plane] = new_image
+        moment_out[0, plane] = vel[1, plane, inner, :]
+        update_out[plane] = templates[0, plane] - learn_rate * (new_image - subjects[0, plane])
+
+
+def last_step(smoothed, image, moment, templates, subjects, smooth_z, inner, step):
+    planes, own = templates.shape[1:3]
+    vmem = pl.BlockSpec(memory_space=pltpu.VMEM)
+    out = jax.ShapeDtypeStruct(templates.shape, jnp.float32)
+    return pl.pallas_call(
+        functools.partial(last_kernel, planes, own, step),
+        out_shape=(out, out, jax.ShapeDtypeStruct(templates.shape[1:], jnp.float32)),
+        in_specs=[pl.BlockSpec(memory_space=pltpu.SMEM)] * 2 + [vmem] * 5,
+        out_specs=(vmem, vmem, vmem),
+        scratch_shapes=[pltpu.VMEM(smoothed.shape, jnp.float32)],
+        compiler_params=pltpu.CompilerParams(vmem_limit_bytes=40 * 2**20),
+    )(inner, smooth_z, smoothed, image, moment, templates, subjects)
+
+
+def matrix_scratch(rows, inner, cols):
+    kinds = [(rows, inner), (rows, inner), (cols, cols), (cols, cols)]
+    return [pltpu.VMEM(kind, jnp.bfloat16) for kind in kinds]
+
+
+def whole_spec(shape):
+    return pl.BlockSpec(shape, lambda at: (0,) * len(shape), pipeline_mode=pl.Buffered(1))
+
+
+def on_device_gathered(templates, momentum, subjects, smooth_x, smooth_y, smooth_z, owned_block):
+    time_step = 1.0 / STEPS
+    planes, own = templates.shape[1:3]
+    total = smooth_y.shape[0]
+    index = lax.axis_index("slab")
+    ends = [planes * cut // 8 for cut in CUTS] + [planes]
+    starts = [0] + ends[:-1]
+    cols_matrix = smooth_x.T
+    chunks, smoothed, done = [], [], 0
+    for start, end in zip(starts, ends):
+        both = jnp.concatenate([templates[:, start:end], momentum[:, start:end]], axis=0)
+        chunks.append(lax.all_gather(both, "slab", axis=2, tiled=True))
+    for at, end in enumerate(ends):
+        ready = end if end == planes else end - 1
+        smoothed.append(
+            chunk_smooth(
+                chunks[: at + 1], starts[: at + 1], done, ready - done, planes, smooth_y, cols_matrix
+            )
+        )
+        done = ready
+    span = own + 2 * EDGE
+    first = jnp.clip(index * own - EDGE, 0, total - span).astype(jnp.int32)
+    inner = (index * own - first).astype(jnp.int32)
+    vel, image, moment = shoot(
+        chunks, starts, smoothed, planes, smooth_z, rows_of(smooth_y, first, span), cols_matrix,
+        first[None], time_step,
+    )
+    image, moment, update = last_step(
+        vel, image, moment, templates, subjects, smooth_z, inner[None], time_step
+    )
+    return (image, moment) + pull(update, owned_block)
+
+
 def on_device(templates, momentum, subjects, smooth_x, smooth_y, smooth_z, owned_block):
-    groups = lax.axis_size("grp")
     time_step = 1.0 / STEPS
     image = templates[0]
     moment = momentum[0]
@@ -74,19 +421,33 @@
         )
         image = new_image
         moment = new_moment
+    return finish(image, moment, templates, subjects, owned_block)
+
+
+def finish(image, moment, templates, subjects, owned_block):
     update = templates[0] - learn_rate * (image - subjects[0])
+    return (image[None], moment[None]) + pull(update, owned_block)
+
+
+def pull(update, owned_block):
+    groups = lax.axis_size("grp")
     planes_all = update.shape[0]
     block_planes = planes_all // groups
     center = lax.psum(update, "grp") / groups
     owned_index = owned_block[lax.axis_index("grp")]
     owned_out = lax.dynamic_slice_in_dim(center, owned_index * block_planes, block_planes, 0)[None]
     new_template = update + pull_weight * (center - update)
-    return (image[None], moment[None], owned_out, new_template[None])
+    return (owned_out, new_template[None])
 
 
 def solution(mesh):
+    def body(*args):
+        templates, smooth_y = args[0], args[4]
+        gathered = 2 * 4 * templates.shape[1] * templates.shape[3] * smooth_y.shape[0]
+        return (on_device_gathered if gathered <= GATHER_BYTES else on_device)(*args)
+
     return jax.shard_map(
-        on_device,
+        body,
         mesh=mesh,
         in_specs=(
             P("grp", None, "slab", None),

time: 474 us -> 369 us (0.78); the launches traced: 468 us -> 369 us
  blocking collectives: 307 us -> 0 us
  waiting for transfers between devices: 38 us -> 180 us
  Pallas kernels: 0 us -> 138 us
  matrix products: 30.9 us -> 0 us
  starting transfers between devices: 17.5 us -> 0.21 us
  other arithmetic: 20.2 us -> 6.12 us
  local copies, waits for them, and re-layouts: 38.9 us -> 29.5 us
    all_to_all x4 -> x0, blocking collectives: 307 us -> none  [the longest x2 156 us: on_device(): lax.all_to_all(pushing, 'slab', split_axis=1, concat_axis=2, tiled=True)]
    pallas_call x0 -> x6, Pallas kernels: none -> 138 us  [the longest x1 69 us: shoot(): pl.pallas_call(functools.partial(shoot_kernel, planes, starts, parts, blo...]
    all_gather x0 -> x4, waiting for transfers between devices: none -> 129 us  [on_device_gathered(): chunks.append(lax.all_gather(both, 'slab', axis=2, tiled=True))]
    dot_general x6 -> x0, matrix products: 30.9 us -> none  [the longest x2 13.6 us: smooth_plane(): jnp.einsum('ij,cpjx->cpix', smooth_y, along, precision=lax.Precision.HIGH...]
    ppermute x8 -> x0, starting transfers between devices: 17.5 us -> none  [the longest x4 12.3 us: with_halo(): lax.ppermute(tail, axis, [(i, (i + 1) % count) for i in range(ends)])]
    neg x2 -> x0, local copies, waits for them, and re-layouts: 17.1 us -> none  [on_device(): plane_vel = -smooth_plane(plane_fields, smooth_x, smooth_y)]
    psum x1, waiting for transfers between devices: 37.1 us -> 50.9 us  [pull(): center = lax.psum(update, 'grp') / groups]
    unnamed x28 -> x35, local copies, waits for them, and re-layouts: 10.6 us -> 24.1 us
  transfers between devices with their start and end apart: 9 -> 5, of which waited for: 2 -> 5; matrix products, arithmetic and copies ran while one was open for 2% -> 2% of each run, Pallas kernels for 0% -> 12%
where the time goes in v2:
time: 369 us
  waiting for transfers between devices  180 us (49%)
  Pallas kernels  138 us (37%)
  local copies, waits for them, and re-layouts  29.5 us (8%)
  between operations  14.7 us (4%)
  other arithmetic  6.12 us (2%)
    all_gather x4, waiting for transfers between devices, on_device_gathered(): chunks.append(lax.all_gather(both, 'slab', axis=2, tiled=True))  129 us
    pallas_call x1, Pallas kernels, shoot(): pl.pallas_call(functools.partial(shoot_kernel, planes, starts, parts, blo...  69 us
    pallas_call x4, Pallas kernels, chunk_smooth(): pl.pallas_call(functools.partial(chunk_kernel, low, count, planes, starts...  60.8 us
    psum x1, waiting for transfers between devices, pull(): center = lax.psum(update, 'grp') / groups  50.9 us
    unnamed x35, local copies, waits for them, and re-layouts  24.1 us
    pallas_call x1, Pallas kernels, last_step(): pl.pallas_call(functools.partial(last_kernel, planes, own, step), out_sha...  8.23 us
  transfers between devices with their start and end apart: 5, of which 5 were waited for; matrix products, arithmetic and copies ran while one was open for 2% of the time, Pallas kernels for 12%

profile of v2, /device:TPU:0, one launch (start us, length us, event | category | flops | bytes accessed | tf_op | source)
XLA Modules:
  0.0 368.7 jit_solution(655531995229363769)
XLA Ops:
  7.2 0.0 copy-start.2
  7.2 0.0 all-gather.5.cloned.1.call-start
  7.2 1.1 slice.25
  8.3 1.0 slice.24
  9.4 0.0 slice-start
  9.4 0.0 slice-start.1
  9.4 0.9 pad_maximum_fusion
  10.3 0.0 all-gather.5.cloned.1.call-update
  10.3 0.0 copy-start.14
  10.4 0.0 all-gather.7.cloned.1.call-start
  10.4 1.2 fusion
  11.6 0.8 pad_maximum_fusion.1
  12.5 0.0 all-gather.7.cloned.1.call-update
  12.5 0.0 all-gather.9.cloned.1.call-start
  12.5 0.8 pad_maximum_fusion.2
  13.4 0.0 all-gather.9.cloned.1.call-update
  13.4 0.0 all-gather.11.cloned.1.call-start
  13.5 0.7 pad_maximum_fusion.3
  14.2 0.0 all-gather.11.cloned.1.call-update
  14.2 0.0 all-reduce.2.cloned.1.call-start
  14.3 1.6 copy.11
  15.9 0.8 constant_dynamic-slice_fusion.refs_8_
  16.6 61.3 %all-gather.5.cloned.1.call-done.refs_0_ = f32[2,3,512,512]{3,2,1,0:T(8,128)} async-done(((f32[2,3,64,512]{3,2,1,0:T(8,128)}), f32[2,3,512,512]{3,2,1,0:T(8,128)}) %all-gather.5.cloned.1.call-update) | async-done | bytes 6291472 | tf_op jit(solution)/shard_map/all_gather | solution.py:377
  77.9 15.1 %shard_map.102.refs_4_ = f32[3,2,512,512]{3,2,1,0:T(8,128)S(1)} custom-call(f32[2,3,512,512]{3,2,1,0:T(8,128)} %all-gather.5.cloned.1.call-done.refs_0_, f32[512,512]{1,0:T(8,128)S(1)} %copy-done.14, f32[512,512]{1,0:T(8,128)S(1)} %bitcast.8), custom_call_target="tpu_custom_call" | custom-call | flops 9663676416 | bytes 10485760 | tf_op jit(solution)/shard_map/pallas_call | solution.py:157
  93.1 2.6 copy-done
  95.7 30.2 %all-gather.7.cloned.1.call-done.refs_1_ = f32[2,2,512,512]{3,2,1,0:T(8,128)} async-done(((f32[2,2,64,512]{3,2,1,0:T(8,128)}), f32[2,2,512,512]{3,2,1,0:T(8,128)}) %all-gather.7.cloned.1.call-update) | async-done | bytes 4194320 | tf_op jit(solution)/shard_map/all_gather | solution.py:377
  125.9 2.2 copy-done.3
  128.1 15.1 %shard_map.103.refs_5_ = f32[3,2,512,512]{3,2,1,0:T(8,128)S(1)} custom-call(f32[2,3,512,512]{3,2,1,0:T(8,128)} %all-gather.5.cloned.1.call-done.refs_0_, f32[2,2,512,512]{3,2,1,0:T(8,128)S(1)} %copy-done.3, f32[512,512]{1,0:T(8,128)S(1)} %copy-done.14, f32[512,512]{1,0:T(8,128)S(1)} %bitcast.9), custom_call_target="tpu_custom_call" | custom-call | flops 9663676416 | bytes 10485760 | tf_op jit(solution)/shard_map/pallas_call | solution.py:157
  143.3 2.6 copy-done.1
  145.8 27.6 %all-gather.9.cloned.1.call-done.refs_2_ = f32[2,2,512,512]{3,2,1,0:T(8,128)} async-done(((f32[2,2,64,512]{3,2,1,0:T(8,128)}), f32[2,2,512,512]{3,2,1,0:T(8,128)}) %all-gather.9.cloned.1.call-update) | async-done | bytes 4194320 | tf_op jit(solution)/shard_map/all_gather | solution.py:377
  173.5 2.2 copy-done.4
  175.7 2.2 copy-done.6
  177.8 15.4 %shard_map.104.refs_6_ = f32[3,2,512,512]{3,2,1,0:T(8,128)} custom-call(f32[2,3,512,512]{3,2,1,0:T(8,128)} %all-gather.5.cloned.1.call-done.refs_0_, f32[2,2,512,512]{3,2,1,0:T(8,128)S(1)} %copy-done.4, f32[2,2,512,512]{3,2,1,0:T(8,128)S(1)} %copy-done.6, f32[512,512]{1,0:T(8,128)S(1)} %copy-done.14, f32[512,512]{1,0:T(8,128)S(1)} %bitcast.10), custom_call_target="tpu_custom_call" | custom-call | flops 9663676416 | bytes 10485760 | tf_op jit(solution)/shard_map/pallas_call | solution.py:157
  193.2 10.2 %all-gather.11.cloned.1.call-done.refs_3_ = f32[2,1,512,512]{3,2,1,0:T(8,128)} async-done(((f32[2,1,64,512]{3,2,1,0:T(8,128)}), f32[2,1,512,512]{3,2,1,0:T(8,128)}) %all-gather.11.cloned.1.call-update) | async-done | bytes 2097168 | tf_op jit(solution)/shard_map/all_gather | solution.py:377
  203.4 2.2 copy-done.5
  205.6 2.2 copy-done.7
  207.8 1.6 copy-done.10
  209.3 15.1 %shard_map.105.refs_7_ = f32[3,2,512,512]{3,2,1,0:T(8,128)} custom-call(f32[2,3,512,512]{3,2,1,0:T(8,128)} %all-gather.5.cloned.1.call-done.refs_0_, f32[2,2,512,512]{3,2,1,0:T(8,128)S(1)} %copy-done.5, f32[2,2,512,512]{3,2,1,0:T(8,128)S(1)} %copy-done.7, f32[2,1,512,512]{3,2,1,0:T(8,128)S(1)} %copy-done.10, f32[512,512]{1,0:T(8,128)S(1)} %copy-done.14, ...), custom_call_target="tpu_custom_call" | custom-call | flops 9663676416 | bytes 10485760 | tf_op jit(solution)/shard_map/pallas_call | solution.py:157
  224.5 69.0 %shard_map.106 = (f32[3,8,80,512]{3,2,1,0:T(8,128)}, f32[8,80,512]{2,1,0:T(8,128)}, f32[8,80,512]{2,1,0:T(8,128)}) custom-call(s32[1]{0:T(128)} %bitcast.1.first_ref, f32[8,8]{1,0:T(8,128)} %smooth_z.3, f32[2,3,512,512]{3,2,1,0:T(8,128)} %all-gather.5.cloned.1.call-done.refs_0_, f32[2,2,512,512]{3,2,1,0:T(8,128)} %all-gather.7.cloned.1.call-done.refs_1_, ...), custom_call_target="tpu_custom_call" | custom-call | tf_op jit(solution)/shard_map/pallas_call | solution.py:277
  293.5 2.1 copy-done.9
  295.6 1.3 copy-done.11
  296.9 1.3 copy-done.12
  298.2 8.2 %shard_map.107 = (f32[1,8,64,512]{3,2,1,0:T(8,128)}, f32[1,8,64,512]{3,2,1,0:T(8,128)}, f32[8,64,512]{2,1,0:T(8,128)}) custom-call(s32[1]{0:T(128)} %bitcast.inner_ref, f32[8,8]{1,0:T(8,128)S(1)} %copy-done.15, f32[3,8,80,512]{3,2,1,0:T(8,128)S(1)} %copy-done.9, f32[8,80,512]{2,1,0:T(8,128)S(1)} %copy-done.11, f32[8,80,512]{2,1,0:T(8,128)S(1)} %copy-done.12, ...), custom_call_target="tpu_custom_call" | custom-call | tf_op jit(solution)/shard_map/pallas_call | solution.py:347
  306.5 0.0 all-reduce.2.cloned.1.call-update
  306.5 0.6 dynamic_slice.10
  307.8 50.9 %all-reduce.2.cloned.1.call-done = f32[8,64,512]{2,1,0:T(8,128)} async-done(((f32[8,64,512]{2,1,0:T(8,128)}), f32[8,64,512]{2,1,0:T(8,128)}) %all-reduce.2.cloned.1.call-update) | async-done | bytes 1048592 | tf_op jit(solution)/shard_map/psum | solution.py:436
  358.7 2.8 add_bitcast_fusion
  361.5 0.7 dynamic-slice_bitcast_fusion
  (23 shorter events, 0.1 us)
Async XLA Ops:
  7.2 3.2 copy-start.2
  7.2 70.7 %all-gather.5.cloned.1.call-start = ((), (), s32[]{:S(2)}) async-start(), calls=%async_computation | async-start | bytes 7077888 | tf_op jit(solution)/shard_map/all_gather | solution.py:377
  9.4 4.1 %slice-start = ((f32[1,8,64,512]{3,2,1,0:T(8,128)}), f32[1,1,64,512]{3,2,1,0:T(8,128)S(1)}, s32[]{:S(2)}) async-start(f32[1,8,64,512]{3,2,1,0:T(8,128)} %templates.1), calls=%async_computation.5 | async-start | bytes 262144 | tf_op jit(solution)/shard_map/slice | solution.py:376
  9.4 4.1 %slice-start.1 = ((f32[1,8,64,512]{3,2,1,0:T(8,128)}), f32[1,1,64,512]{3,2,1,0:T(8,128)S(1)}, s32[]{:S(2)}) async-start(f32[1,8,64,512]{3,2,1,0:T(8,128)} %param.8), calls=%async_computation.6 | async-start | bytes 262144 | tf_op jit(solution)/shard_map/slice | solution.py:376
  10.3 5.5 %copy-start.14 = (f32[512,512]{1,0:T(8,128)S(1)}, f32[512,512]{1,0:T(8,128)}, u32[]{:S(2)}) copy-start(f32[512,512]{1,0:T(8,128)} %refs_4_.1) | copy-start | bytes 3145732
  10.4 115.6 %all-gather.7.cloned.1.call-start = ((), (), s32[]{:S(2)}) async-start(), calls=%async_computation.1 | async-start | bytes 4718592 | tf_op jit(solution)/shard_map/all_gather | solution.py:377
  12.5 161.0 %all-gather.9.cloned.1.call-start = ((), (), s32[]{:S(2)}) async-start(), calls=%async_computation.2 | async-start | bytes 4718592 | tf_op jit(solution)/shard_map/all_gather | solution.py:377
  13.4 190.0 %all-gather.11.cloned.1.call-start = ((), (), s32[]{:S(2)}) async-start(), calls=%async_computation.3 | async-start | bytes 2359296 | tf_op jit(solution)/shard_map/all_gather | solution.py:377
  14.2 344.5 %all-reduce.2.cloned.1.call-start = ((), (), s32[]{:S(2)}) async-start(), calls=%async_computation.4 | async-start | bytes 2097152 | tf_op jit(solution)/shard_map/psum | solution.py:436
  15.8 187.5 %copy-start.8 = (f32[512,512]{0,1:T(8,128)}, f32[512,512]{0,1:T(8,128)S(1)}, u32[]{:S(2)}) copy-start(f32[512,512]{0,1:T(8,128)S(1)} %copy.11) | copy-start | bytes 3145732
  93.0 2.6 copy-start
  125.9 2.2 copy-start.3
  143.2 2.6 copy-start.1
  173.5 2.2 copy-start.4
  175.7 2.2 copy-start.6
  203.4 2.2 copy-start.5
  205.6 2.2 copy-start.7
  207.7 1.6 copy-start.10
  224.5 69.0 %copy-start.13 = (f32[1,8,64,512]{3,2,1,0:T(8,128)S(1)}, f32[1,8,64,512]{3,2,1,0:T(8,128)}, u32[]{:S(2)}) copy-start(f32[1,8,64,512]{3,2,1,0:T(8,128)} %subjects.1) | copy-start | bytes 3145732
  224.5 69.0 %copy-start.15 = (f32[8,8]{1,0:T(8,128)S(1)}, f32[8,8]{1,0:T(8,128)}, u32[]{:S(2)}) copy-start(f32[8,8]{1,0:T(8,128)} %smooth_z.3) | copy-start | bytes 772
  293.5 2.1 copy-start.9
  295.6 1.3 copy-start.11
  296.9 1.3 copy-start.12
  298.2 8.3 %copy-start.16 = (s32[4]{0:T(128)S(1)}, s32[4]{0:T(128)}, u32[]{:S(2)}) copy-start(s32[4]{0:T(128)} %param.13) | copy-start | bytes 52
Sparse Core Ops, SparseCore 0:
  10.5 67.4 all-gather.4
  80.1 45.7 all-gather.6
  127.5 45.9 all-gather.8
  175.5 27.8 all-gather.10
  306.6 52.0 all-reduce.1

commit v3 on v2

--- a/solution.py
+++ b/solution.py
@@ -9,7 +9,7 @@
 
 STEPS = 2
 EDGE = 8
-CUTS = (3, 5, 7)
+CUTS = (6,)
 VMEM_BYTES = 60 * 2**20
 GATHER_BYTES = 16 * 2**20
 
@@ -73,6 +73,10 @@
 
 def dot3(left, right):
     mul = lambda a, b: jnp.dot(a, b, preferred_element_type=jnp.float32)
+    rows = left[0].shape[0]
+    if rows <= 128:
+        both = mul(jnp.concatenate(left, axis=0), right[0])
+        return both[:rows] + (mul(left[0], right[1]) + both[rows:])
     return mul(left[0], right[0]) + (mul(left[0], right[1]) + mul(left[1], right[0]))
 
 
@@ -173,7 +177,7 @@
             bytes_accessed=20 * count * rows * cols,
             transcendentals=0,
         ),
-        compiler_params=pltpu.CompilerParams(vmem_limit_bytes=40 * 2**20),
+        compiler_params=pltpu.CompilerParams(vmem_limit_bytes=VMEM_BYTES),
     )(*chunks, smooth_y, cols_matrix)
 
 
@@ -429,11 +433,27 @@
     return (image[None], moment[None]) + pull(update, owned_block)
 
 
+def sum_groups(field, orders):
+    groups = lax.axis_size("grp")
+    share = field.shape[0] // len(orders)
+    pieces = [field[at * share : (at + 1) * share] for at in range(len(orders))]
+    for turn in range(len(orders[0])):
+        sent = [
+            lax.ppermute(piece, "grp", [(i, i ^ order[turn]) for i in range(groups)])
+            for piece, order in zip(pieces, orders)
+        ]
+        pieces = [piece + got for piece, got in zip(pieces, sent)]
+    return jnp.concatenate(pieces, axis=0)
+
+
 def pull(update, owned_block):
     groups = lax.axis_size("grp")
     planes_all = update.shape[0]
     block_planes = planes_all // groups
-    center = lax.psum(update, "grp") / groups
+    if groups == 4 and planes_all % 2 == 0:
+        center = sum_groups(update, ((1, 2), (2, 1))) / groups
+    else:
+        center = lax.psum(update, "grp") / groups
     owned_index = owned_block[lax.axis_index("grp")]
     owned_out = lax.dynamic_slice_in_dim(center, owned_index * block_planes, block_planes, 0)[None]
     new_template = update + pull_weight * (center - update)

time: 369 us -> 318 us (0.86)
  waiting for transfers between devices: 180 us -> 148 us
  local copies, waits for them, and re-layouts: 29.5 us -> 11.3 us
  starting transfers between devices: 0.21 us -> 5.22 us
  Pallas kernels: 138 us -> 134 us
    psum x1 -> x0, waiting for transfers between devices: 50.9 us -> none  [pull(): center = lax.psum(update, 'grp') / groups]
    ppermute x0 -> x4, waiting for transfers between devices: none -> 23.1 us  [sum_groups(): lax.ppermute(piece, 'grp', [(i, i ^ order[turn]) for i in range(groups)])]
    unnamed x35 -> x17, local copies, waits for them, and re-layouts: 24.1 us -> 6.07 us
    ppermute x0 -> x4, starting transfers between devices: none -> 5.14 us  [sum_groups(): lax.ppermute(piece, 'grp', [(i, i ^ order[turn]) for i in range(groups)])]
    pallas_call x1, Pallas kernels: 69 us -> 64.4 us  [shoot(): pl.pallas_call(functools.partial(shoot_kernel, planes, starts, parts, blo...]
    all_gather x4 -> x2, waiting for transfers between devices: 129 us -> 125 us  [on_device_gathered(): chunks.append(lax.all_gather(both, 'slab', axis=2, tiled=True))]
    pallas_call x4 -> x2, Pallas kernels: 60.8 us -> 62.2 us  [chunk_smooth(): pl.pallas_call(functools.partial(chunk_kernel, low, count, planes, starts...]
  transfers between devices with their start and end apart: 5 -> 6, of which waited for: 5 -> 6; matrix products, arithmetic and copies ran while one was open for 2% -> 1% of each run, Pallas kernels for 12% -> 12%
where the time goes in v3:
time: 318 us
  waiting for transfers between devices  148 us (47%)
  Pallas kernels  134 us (42%)
  between operations  14.8 us (5%)
  local copies, waits for them, and re-layouts  11.3 us (4%)
  starting transfers between devices  5.22 us (2%)
  other arithmetic  3.88 us (1%)
    all_gather x2, waiting for transfers between devices, on_device_gathered(): chunks.append(lax.all_gather(both, 'slab', axis=2, tiled=True))  125 us
    pallas_call x1, Pallas kernels, shoot(): pl.pallas_call(functools.partial(shoot_kernel, planes, starts, parts, blo...  64.4 us
    pallas_call x2, Pallas kernels, chunk_smooth(): pl.pallas_call(functools.partial(chunk_kernel, low, count, planes, starts...  62.2 us
    ppermute x4, waiting for transfers between devices, sum_groups(): lax.ppermute(piece, 'grp', [(i, i ^ order[turn]) for i in range(groups)])  23.1 us
    pallas_call x1, Pallas kernels, last_step(): pl.pallas_call(functools.partial(last_kernel, planes, own, step), out_sha...  7.88 us
  transfers between devices with their start and end apart: 6, of which 6 were waited for; matrix products, arithmetic and copies ran while one was open for 1% of the time, Pallas kernels for 12%

profile of v3, /device:TPU:0, one launch (start us, length us, event | category | flops | bytes accessed | tf_op | source)
XLA Modules:
  0.0 317.7 jit_solution(575423953781380988)
XLA Ops:
  7.2 0.0 slice-start.2
  7.2 0.0 slice-start
  7.2 0.0 all-gather.3.cloned.1.call-start
  7.2 1.1 slice-done.2
  8.3 0.2 slice-done
  8.5 1.4 pad_maximum_fusion
  10.0 0.0 all-gather.3.cloned.1.call-update
  10.0 0.0 copy-start.6
  10.0 0.0 all-gather.5.cloned.1.call-start
  10.1 0.9 slice-done.1
  10.9 0.1 slice-done.3
  11.0 0.8 pad_maximum_fusion.1
  11.9 0.0 all-gather.5.cloned.1.call-update
  11.9 0.0 copy-done.6
  11.9 1.3 copy.11
  13.2 1.6 constant_dynamic-slice_fusion.refs_4_
  14.8 114.8 %all-gather.3.cloned.1.call-done.refs_0_ = f32[2,6,512,512]{3,2,1,0:T(8,128)} async-done(((f32[2,6,64,512]{3,2,1,0:T(8,128)}), f32[2,6,512,512]{3,2,1,0:T(8,128)}) %all-gather.3.cloned.1.call-update) | async-done | bytes 12582928 | tf_op jit(solution)/shard_map/all_gather | solution.py:381
  129.6 37.5 %shard_map.102.refs_2_ = f32[3,5,512,512]{3,2,1,0:T(8,128)} custom-call(f32[2,6,512,512]{3,2,1,0:T(8,128)} %all-gather.3.cloned.1.call-done.refs_0_, f32[512,512]{1,0:T(8,128)} %refs_2_.1, f32[512,512]{1,0:T(8,128)} %bitcast.8), custom_call_target="tpu_custom_call" | custom-call | flops 24159191040 | bytes 26214400 | tf_op jit(solution)/shard_map/pallas_call | solution.py:161
  167.1 10.0 %all-gather.5.cloned.1.call-done.refs_1_ = f32[2,2,512,512]{3,2,1,0:T(8,128)} async-done(((f32[2,2,64,512]{3,2,1,0:T(8,128)}), f32[2,2,512,512]{3,2,1,0:T(8,128)}) %all-gather.5.cloned.1.call-update) | async-done | bytes 4194320 | tf_op jit(solution)/shard_map/all_gather | solution.py:381
  177.1 24.7 %shard_map.103.refs_3_ = f32[3,3,512,512]{3,2,1,0:T(8,128)} custom-call(f32[2,6,512,512]{3,2,1,0:T(8,128)} %all-gather.3.cloned.1.call-done.refs_0_, f32[2,2,512,512]{3,2,1,0:T(8,128)} %all-gather.5.cloned.1.call-done.refs_1_, f32[512,512]{1,0:T(8,128)} %refs_2_.1, f32[512,512]{1,0:T(8,128)} %bitcast.9), custom_call_target="tpu_custom_call" | custom-call | flops 14495514624 | bytes 15728640 | tf_op jit(solution)/shard_map/pallas_call | solution.py:161
  201.8 0.0 copy-start
  201.9 0.0 copy-start.4
  201.9 0.0 copy-start.5
  201.9 64.4 %shard_map.104 = (f32[3,8,80,512]{3,2,1,0:T(8,128)}, f32[8,80,512]{2,1,0:T(8,128)}, f32[8,80,512]{2,1,0:T(8,128)}) custom-call(s32[1]{0:T(128)} %bitcast.1.first_ref, f32[8,8]{1,0:T(8,128)} %smooth_z.3, f32[2,6,512,512]{3,2,1,0:T(8,128)} %all-gather.3.cloned.1.call-done.refs_0_, f32[2,2,512,512]{3,2,1,0:T(8,128)} %all-gather.5.cloned.1.call-done.refs_1_, ...), custom_call_target="tpu_custom_call" | custom-call | tf_op jit(solution)/shard_map/pallas_call | solution.py:281
  266.3 0.0 copy-done
  266.3 0.0 copy-done.4
  266.3 0.0 copy-done.5
  266.3 0.0 copy-start.1
  266.3 2.1 copy-done.1
  268.4 1.3 copy-done.2
  269.7 1.3 copy-done.3
  271.0 7.9 %shard_map.105 = (f32[1,8,64,512]{3,2,1,0:T(8,128)}, f32[1,8,64,512]{3,2,1,0:T(8,128)}, f32[8,64,512]{2,1,0:T(8,128)S(1)}) custom-call(s32[1]{0:T(128)} %bitcast.inner_ref, f32[8,8]{1,0:T(8,128)S(1)} %copy-done.5, f32[3,8,80,512]{3,2,1,0:T(8,128)S(1)} %copy-done.1, f32[8,80,512]{2,1,0:T(8,128)S(1)} %copy-done.2, f32[8,80,512]{2,1,0:T(8,128)S(1)} %copy-done.3, ...), custom_call_target="tpu_custom_call" | custom-call | tf_op jit(solution)/shard_map/pallas_call | solution.py:351
  278.9 0.1 fusion
  279.0 1.6 collective-permute-start
  280.6 1.5 collective-permute-start.2
  282.1 11.1 %collective-permute-done = f32[4,64,512]{2,1,0:T(8,128)S(1)} collective-permute-done((f32[4,64,512]{2,1,0:T(8,128)S(1)}, f32[4,64,512]{2,1,0:T(8,128)S(1)}, u32[]{:S(2)}, u32[]{:S(2)}) %collective-permute-start) | collective-permute-done | bytes 524320 | tf_op jit(solution)/shard_map/ppermute | solution.py:442
  293.2 1.3 collective-permute-done.2
  294.4 0.2 slice_add_fusion.1
  294.6 1.5 collective-permute-start.1
  296.2 0.6 collective-permute-start.3
  296.7 0.0 copy-done.7
  296.7 0.6 dynamic_slice.10
  298.0 9.7 %collective-permute-done.1 = f32[4,64,512]{2,1,0:T(8,128)S(1)} collective-permute-done((f32[4,64,512]{2,1,0:T(8,128)S(1)}, f32[4,64,512]{2,1,0:T(8,128)S(1)}, u32[]{:S(2)}, u32[]{:S(2)}) %collective-permute-start.1) | collective-permute-done | bytes 524320 | tf_op jit(solution)/shard_map/ppermute | solution.py:442
  307.7 0.1 add.24
  307.7 1.1 collective-permute-done.3
  308.9 0.1 add.26
  308.9 1.2 add_bitcast_fusion
  310.2 0.7 dynamic-slice_bitcast_fusion
  (5 shorter events, 0.0 us)
Async XLA Ops:
  7.2 1.1 slice-start.2
  7.2 1.4 slice-start
  7.2 122.4 %all-gather.3.cloned.1.call-start = ((), (), s32[]{:S(2)}) async-start(), calls=%async_computation | async-start | bytes 14155776 | tf_op jit(solution)/shard_map/all_gather | solution.py:381
  10.0 0.9 slice-start.1
  10.0 1.0 slice-start.3
  10.0 1.9 copy-start.6
  10.0 167.1 %all-gather.5.cloned.1.call-start = ((), (), s32[]{:S(2)}) async-start(), calls=%async_computation.1 | async-start | bytes 4718592 | tf_op jit(solution)/shard_map/all_gather | solution.py:381
  201.8 64.4 %copy-start = (f32[1,8,64,512]{3,2,1,0:T(8,128)S(1)}, f32[1,8,64,512]{3,2,1,0:T(8,128)}, u32[]{:S(2)}) copy-start(f32[1,8,64,512]{3,2,1,0:T(8,128)} %templates.1) | copy-start | bytes 3145732
  201.9 64.4 %copy-start.4 = (f32[1,8,64,512]{3,2,1,0:T(8,128)S(1)}, f32[1,8,64,512]{3,2,1,0:T(8,128)}, u32[]{:S(2)}) copy-start(f32[1,8,64,512]{3,2,1,0:T(8,128)} %subjects.1) | copy-start | bytes 3145732
  201.9 64.4 %copy-start.5 = (f32[8,8]{1,0:T(8,128)S(1)}, f32[8,8]{1,0:T(8,128)}, u32[]{:S(2)}) copy-start(f32[8,8]{1,0:T(8,128)} %smooth_z.3) | copy-start | bytes 772
  266.3 2.1 copy-start.1
  268.4 1.3 copy-start.2
  269.7 1.3 copy-start.3
  279.0 14.1 %collective-permute-start = (f32[4,64,512]{2,1,0:T(8,128)S(1)}, f32[4,64,512]{2,1,0:T(8,128)S(1)}, u32[]{:S(2)}, u32[]{:S(2)}) collective-permute-start(f32[4,64,512]{2,1,0:T(8,128)S(1)} %get-tuple-element.20), channel_id=1, source_target_pairs={{0,8},{8,0},{16,24},{24,16},{1,9},{9,1},{17,25},{25,17},{2,10},{10... | collective-permute-start | bytes 1572872 | tf_op jit(solution)/shard_map/ppermute | solution.py:442
  280.6 16.1 %copy-start.7 = (s32[4]{0:T(128)S(1)}, s32[4]{0:T(128)}, u32[]{:S(2)}) copy-start(s32[4]{0:T(128)} %param.13) | copy-start | bytes 52
  280.6 13.8 %collective-permute-start.2 = (f32[4,64,512]{2,1,0:T(8,128)S(1)}, f32[4,64,512]{2,1,0:T(8,128)S(1)}, u32[]{:S(2)}, u32[]{:S(2)}) collective-permute-start(f32[4,64,512]{2,1,0:T(8,128)S(1)} %get-tuple-element.21), channel_id=1, source_target_pairs={{0,16},{8,24},{16,0},{24,8},{1,17},{9,25},{17,1},{25,9},{2,18},{10... | collective-permute-start | bytes 1572872 | tf_op jit(solution)/shard_map/ppermute | solution.py:442
  294.6 13.0 %collective-permute-start.1 = (f32[4,64,512]{2,1,0:T(8,128)S(1)}, f32[4,64,512]{2,1,0:T(8,128)S(1)}, u32[]{:S(2)}, u32[]{:S(2)}) collective-permute-start(f32[4,64,512]{2,1,0:T(8,128)S(1)} %get-tuple-element.18), channel_id=1, source_target_pairs={{0,16},{8,24},{16,0},{24,8},{1,17},{9,25},{17,1},{25,9},{2,18},{10... | collective-permute-start | bytes 1572872 | tf_op jit(solution)/shard_map/ppermute | solution.py:442
  296.2 12.7 %collective-permute-start.3 = (f32[4,64,512]{2,1,0:T(8,128)S(1)}, f32[4,64,512]{2,1,0:T(8,128)S(1)}, u32[]{:S(2)}, u32[]{:S(2)}) collective-permute-start(f32[4,64,512]{2,1,0:T(8,128)S(1)} %get-tuple-element.19), channel_id=1, source_target_pairs={{0,8},{8,0},{16,24},{24,16},{1,9},{9,1},{17,25},{25,17},{2,10},{10... | collective-permute-start | bytes 1572872 | tf_op jit(solution)/shard_map/ppermute | solution.py:442
Sparse Core Ops, SparseCore 0:
  10.1 119.4 all-gather.2
  131.8 45.2 all-gather.4

commit v4 on v3

--- a/solution.py
+++ b/solution.py
@@ -99,8 +99,7 @@
     for at, grad in enumerate(grads):
         fields[at] = moment * grad
 
-    @pl.loop(0, 3)
-    def _(at):
+    for at in range(3):
         along = dot3((rows_high[...], rows_low[...]), halve(fields[at]))
         store(at, dot3(halve(along), (cols_high[...], cols_low[...])))
 

time: 318 us -> 313 us (0.984)
  Pallas kernels: 134 us -> 125 us
  waiting for transfers between devices: 148 us -> 152 us
    pallas_call x2, Pallas kernels: 62.2 us -> 56 us  [chunk_smooth(): pl.pallas_call(functools.partial(chunk_kernel, low, count, planes, starts...]
    all_gather x2, waiting for transfers between devices: 125 us -> 129 us  [on_device_gathered(): chunks.append(lax.all_gather(both, 'slab', axis=2, tiled=True))]
  transfers between devices with their start and end apart: 6 -> 6, of which waited for: 6 -> 6; matrix products, arithmetic and copies ran while one was open for 1% -> 1% of each run, Pallas kernels for 12% -> 11%
where the time goes in v4:
time: 313 us
  waiting for transfers between devices  152 us (49%)
  Pallas kernels  125 us (40%)
  between operations  14.8 us (5%)
  local copies, waits for them, and re-layouts  11.3 us (4%)
  starting transfers between devices  5.19 us (2%)
  other arithmetic  3.88 us (1%)
    all_gather x2, waiting for transfers between devices, on_device_gathered(): chunks.append(lax.all_gather(both, 'slab', axis=2, tiled=True))  129 us
    pallas_call x1, Pallas kernels, shoot(): pl.pallas_call(functools.partial(shoot_kernel, planes, starts, parts, blo...  61.6 us
    pallas_call x2, Pallas kernels, chunk_smooth(): pl.pallas_call(functools.partial(chunk_kernel, low, count, planes, starts...  56 us
    ppermute x4, waiting for transfers between devices, sum_groups(): lax.ppermute(piece, 'grp', [(i, i ^ order[turn]) for i in range(groups)])  23.1 us
    pallas_call x1, Pallas kernels, last_step(): pl.pallas_call(functools.partial(last_kernel, planes, own, step), out_sha...  7.88 us
  transfers between devices with their start and end apart: 6, of which 6 were waited for; matrix products, arithmetic and copies ran while one was open for 1% of the time, Pallas kernels for 11%

profile of v4, /device:TPU:0, one launch (start us, length us, event | category | flops | bytes accessed | tf_op | source)
XLA Modules:
  0.0 312.6 jit_solution(16369244636066769956)
XLA Ops:
  7.2 0.0 slice-start.2
  7.2 0.0 slice-start
  7.2 0.0 all-gather.3.cloned.1.call-start
  7.2 1.1 slice-done.2
  8.3 0.2 slice-done
  8.5 1.4 pad_maximum_fusion
  10.0 0.0 all-gather.3.cloned.1.call-update
  10.0 0.0 copy-start.6
  10.0 0.0 all-gather.5.cloned.1.call-start
  10.1 0.9 slice-done.1
  10.9 0.1 slice-done.3
  11.0 0.8 pad_maximum_fusion.1
  11.9 0.0 all-gather.5.cloned.1.call-update
  11.9 0.0 copy-done.6
  11.9 1.3 copy.11
  13.2 1.6 constant_dynamic-slice_fusion.refs_4_
  14.8 114.8 %all-gather.3.cloned.1.call-done.refs_0_ = f32[2,6,512,512]{3,2,1,0:T(8,128)} async-done(((f32[2,6,64,512]{3,2,1,0:T(8,128)}), f32[2,6,512,512]{3,2,1,0:T(8,128)}) %all-gather.3.cloned.1.call-update) | async-done | bytes 12582928 | tf_op jit(solution)/shard_map/all_gather | solution.py:380
  129.6 33.6 %shard_map.102.refs_2_ = f32[3,5,512,512]{3,2,1,0:T(8,128)} custom-call(f32[2,6,512,512]{3,2,1,0:T(8,128)} %all-gather.3.cloned.1.call-done.refs_0_, f32[512,512]{1,0:T(8,128)} %refs_2_.1, f32[512,512]{1,0:T(8,128)} %bitcast.8), custom_call_target="tpu_custom_call" | custom-call | flops 24159191040 | bytes 26214400 | tf_op jit(solution)/shard_map/pallas_call | solution.py:160
  163.2 14.0 %all-gather.5.cloned.1.call-done.refs_1_ = f32[2,2,512,512]{3,2,1,0:T(8,128)} async-done(((f32[2,2,64,512]{3,2,1,0:T(8,128)}), f32[2,2,512,512]{3,2,1,0:T(8,128)}) %all-gather.5.cloned.1.call-update) | async-done | bytes 4194320 | tf_op jit(solution)/shard_map/all_gather | solution.py:380
  177.2 22.5 %shard_map.103.refs_3_ = f32[3,3,512,512]{3,2,1,0:T(8,128)} custom-call(f32[2,6,512,512]{3,2,1,0:T(8,128)} %all-gather.3.cloned.1.call-done.refs_0_, f32[2,2,512,512]{3,2,1,0:T(8,128)} %all-gather.5.cloned.1.call-done.refs_1_, f32[512,512]{1,0:T(8,128)} %refs_2_.1, f32[512,512]{1,0:T(8,128)} %bitcast.9), custom_call_target="tpu_custom_call" | custom-call | flops 14495514624 | bytes 15728640 | tf_op jit(solution)/shard_map/pallas_call | solution.py:160
  199.6 0.0 copy-start
  199.6 0.0 copy-start.4
  199.7 0.0 copy-start.5
  199.7 61.6 %shard_map.104 = (f32[3,8,80,512]{3,2,1,0:T(8,128)}, f32[8,80,512]{2,1,0:T(8,128)}, f32[8,80,512]{2,1,0:T(8,128)}) custom-call(s32[1]{0:T(128)} %bitcast.1.first_ref, f32[8,8]{1,0:T(8,128)} %smooth_z.3, f32[2,6,512,512]{3,2,1,0:T(8,128)} %all-gather.3.cloned.1.call-done.refs_0_, f32[2,2,512,512]{3,2,1,0:T(8,128)} %all-gather.5.cloned.1.call-done.refs_1_, ...), custom_call_target="tpu_custom_call" | custom-call | tf_op jit(solution)/shard_map/pallas_call | solution.py:280
  261.2 0.0 copy-done
  261.2 0.0 copy-done.4
  261.3 0.0 copy-done.5
  261.3 0.0 copy-start.1
  261.3 2.1 copy-done.1
  263.4 1.3 copy-done.2
  264.7 1.3 copy-done.3
  266.0 7.9 %shard_map.105 = (f32[1,8,64,512]{3,2,1,0:T(8,128)}, f32[1,8,64,512]{3,2,1,0:T(8,128)}, f32[8,64,512]{2,1,0:T(8,128)S(1)}) custom-call(s32[1]{0:T(128)} %bitcast.inner_ref, f32[8,8]{1,0:T(8,128)S(1)} %copy-done.5, f32[3,8,80,512]{3,2,1,0:T(8,128)S(1)} %copy-done.1, f32[8,80,512]{2,1,0:T(8,128)S(1)} %copy-done.2, f32[8,80,512]{2,1,0:T(8,128)S(1)} %copy-done.3, ...), custom_call_target="tpu_custom_call" | custom-call | tf_op jit(solution)/shard_map/pallas_call | solution.py:350
  273.9 0.1 fusion
  274.0 1.5 collective-permute-start
  275.5 1.5 collective-permute-start.2
  277.0 11.1 %collective-permute-done = f32[4,64,512]{2,1,0:T(8,128)S(1)} collective-permute-done((f32[4,64,512]{2,1,0:T(8,128)S(1)}, f32[4,64,512]{2,1,0:T(8,128)S(1)}, u32[]{:S(2)}, u32[]{:S(2)}) %collective-permute-start) | collective-permute-done | bytes 524320 | tf_op jit(solution)/shard_map/ppermute | solution.py:441
  288.1 1.2 collective-permute-done.2
  289.3 0.2 slice_add_fusion.1
  289.5 1.5 collective-permute-start.1
  291.1 0.6 collective-permute-start.3
  291.6 0.0 copy-done.7
  291.6 0.6 dynamic_slice.10
  292.9 9.6 %collective-permute-done.1 = f32[4,64,512]{2,1,0:T(8,128)S(1)} collective-permute-done((f32[4,64,512]{2,1,0:T(8,128)S(1)}, f32[4,64,512]{2,1,0:T(8,128)S(1)}, u32[]{:S(2)}, u32[]{:S(2)}) %collective-permute-start.1) | collective-permute-done | bytes 524320 | tf_op jit(solution)/shard_map/ppermute | solution.py:441
  302.5 0.1 add.24
  302.6 1.1 collective-permute-done.3
  303.7 0.1 add.26
  303.8 1.2 add_bitcast_fusion
  305.0 0.7 dynamic-slice_bitcast_fusion
  (5 shorter events, 0.0 us)
Async XLA Ops:
  7.2 1.1 slice-start.2
  7.2 1.4 slice-start
  7.2 122.4 %all-gather.3.cloned.1.call-start = ((), (), s32[]{:S(2)}) async-start(), calls=%async_computation | async-start | bytes 14155776 | tf_op jit(solution)/shard_map/all_gather | solution.py:380
  10.0 0.9 slice-start.1
  10.0 1.0 slice-start.3
  10.0 1.9 copy-start.6
  10.0 167.1 %all-gather.5.cloned.1.call-start = ((), (), s32[]{:S(2)}) async-start(), calls=%async_computation.1 | async-start | bytes 4718592 | tf_op jit(solution)/shard_map/all_gather | solution.py:380
  199.6 61.6 %copy-start = (f32[1,8,64,512]{3,2,1,0:T(8,128)S(1)}, f32[1,8,64,512]{3,2,1,0:T(8,128)}, u32[]{:S(2)}) copy-start(f32[1,8,64,512]{3,2,1,0:T(8,128)} %templates.1) | copy-start | bytes 3145732
  199.6 61.6 %copy-start.4 = (f32[1,8,64,512]{3,2,1,0:T(8,128)S(1)}, f32[1,8,64,512]{3,2,1,0:T(8,128)}, u32[]{:S(2)}) copy-start(f32[1,8,64,512]{3,2,1,0:T(8,128)} %subjects.1) | copy-start | bytes 3145732
  199.7 61.6 %copy-start.5 = (f32[8,8]{1,0:T(8,128)S(1)}, f32[8,8]{1,0:T(8,128)}, u32[]{:S(2)}) copy-start(f32[8,8]{1,0:T(8,128)} %smooth_z.3) | copy-start | bytes 772
  261.3 2.1 copy-start.1
  263.4 1.3 copy-start.2
  264.7 1.3 copy-start.3
  274.0 14.1 %collective-permute-start = (f32[4,64,512]{2,1,0:T(8,128)S(1)}, f32[4,64,512]{2,1,0:T(8,128)S(1)}, u32[]{:S(2)}, u32[]{:S(2)}) collective-permute-start(f32[4,64,512]{2,1,0:T(8,128)S(1)} %get-tuple-element.20), channel_id=1, source_target_pairs={{0,8},{8,0},{16,24},{24,16},{1,9},{9,1},{17,25},{25,17},{2,10},{10... | collective-permute-start | bytes 1572872 | tf_op jit(solution)/shard_map/ppermute | solution.py:441
  275.5 16.1 %copy-start.7 = (s32[4]{0:T(128)S(1)}, s32[4]{0:T(128)}, u32[]{:S(2)}) copy-start(s32[4]{0:T(128)} %param.13) | copy-start | bytes 52
  275.5 13.8 %collective-permute-start.2 = (f32[4,64,512]{2,1,0:T(8,128)S(1)}, f32[4,64,512]{2,1,0:T(8,128)S(1)}, u32[]{:S(2)}, u32[]{:S(2)}) collective-permute-start(f32[4,64,512]{2,1,0:T(8,128)S(1)} %get-tuple-element.21), channel_id=1, source_target_pairs={{0,16},{8,24},{16,0},{24,8},{1,17},{9,25},{17,1},{25,9},{2,18},{10... | collective-permute-start | bytes 1572872 | tf_op jit(solution)/shard_map/ppermute | solution.py:441
  289.5 13.0 %collective-permute-start.1 = (f32[4,64,512]{2,1,0:T(8,128)S(1)}, f32[4,64,512]{2,1,0:T(8,128)S(1)}, u32[]{:S(2)}, u32[]{:S(2)}) collective-permute-start(f32[4,64,512]{2,1,0:T(8,128)S(1)} %get-tuple-element.18), channel_id=1, source_target_pairs={{0,16},{8,24},{16,0},{24,8},{1,17},{9,25},{17,1},{25,9},{2,18},{10... | collective-permute-start | bytes 1572872 | tf_op jit(solution)/shard_map/ppermute | solution.py:441
  291.1 12.6 %collective-permute-start.3 = (f32[4,64,512]{2,1,0:T(8,128)S(1)}, f32[4,64,512]{2,1,0:T(8,128)S(1)}, u32[]{:S(2)}, u32[]{:S(2)}) collective-permute-start(f32[4,64,512]{2,1,0:T(8,128)S(1)} %get-tuple-element.19), channel_id=1, source_target_pairs={{0,8},{8,0},{16,24},{24,16},{1,9},{9,1},{17,25},{25,17},{2,10},{10... | collective-permute-start | bytes 1572872 | tf_op jit(solution)/shard_map/ppermute | solution.py:441
Sparse Core Ops, SparseCore 0:
  10.1 119.4 all-gather.2
  131.8 45.3 all-gather.4
